TPU v7x, 512 devices: a whole 4x8x8 slice. The times are simulated.
512 devices in a mesh: wide: 64 (over x, z, core), narrow: 8 (over y).
Axes of the slice: x: 4, y: 8, z: 8, core: 2. Of those that a mesh axis runs over, the one named last changes fastest.
Arguments:
- quot_owner: int32 [262144, 1], P(('wide', 'narrow')), may hold values from 0 to 63; in each aligned block of 512 rows (0 to 511, 512 to 1023, ...) at most 16 rows name the same one
- quot_row: int32 [262144], P(('wide', 'narrow')), may hold values from 0 to 1023
- rem_owner: int32 [262144, 1], P(('wide', 'narrow')), may hold values from 0 to 7, as said below
- rem_row: int32 [262144], P(('wide', 'narrow')), may hold values from 0 to 4095, as said below
- out_grad: bfloat16 [262144, 256], P(('wide', 'narrow')), may hold values from -6 to 6
- quot_table: bfloat16 [65536, 256], P('wide'), may hold values from -127 to 127
- quot_scale: float32 [65536], P('wide'), may hold values from 0.002 to 0.02
- rem_table: bfloat16 [32768, 256], P('narrow'), may hold values from -4 to 4
Outputs:
- grad_quot: float32 [65536, 256], P('wide')
- grad_rem: float32 [8, 4096, 256], P('narrow', 'wide')
Inputs may be any that keep to these rules, and one draw needn't show every extreme that they name: `quot_owner`: of the ids of one device, at most 16 have the same quotient owner, and some device reaches it. `rem_owner`: of the ids of one device, exactly 64 have each remainder owner. Of the ids of one device with the same remainder owner, at most 2 have the same rem_row // 64; for one owner and one such block, drawn from the seed, every device has exactly 2.
All inputs are finite; a program needn't handle non-finite values.
Results may differ from a plain program's by a relative error of at most 0.0041.
Values may be sent and summed in bfloat16 or wider, within the bound.
A program may use at most 64 MiB of HBM per device.

v0:
```python
import jax
import jax.numpy as jnp
from jax import lax
from jax.sharding import PartitionSpec as P


def slot_index(owners, peer_count, capacity):
    matches = (owners[:, None] == jnp.arange(peer_count, dtype=jnp.int32)[None, :]).astype(
        jnp.int32
    )
    before = jnp.cumsum(matches, axis=0) - matches
    return owners * capacity + jnp.sum(before * matches, axis=1)


def pack_rows(values, target, total_slots, filler):
    full_shape = (total_slots,) + values.shape[1:]
    return jnp.full(full_shape, filler, values.dtype).at[target].set(values, mode="drop")


def on_device(
    quot_owner, quot_row, rem_owner, rem_row, out_grad, quot_table, quot_scale, rem_table
):
    wide_size = lax.axis_size("wide")
    narrow_size = lax.axis_size("narrow")
    tokens, width = out_grad.shape
    quot_slots = 2 * tokens // wide_size
    rem_slots = tokens // narrow_size
    quot_target = slot_index(quot_owner[:, 0], wide_size, quot_slots)
    rem_target = slot_index(rem_owner[:, 0], narrow_size, rem_slots)
    quot_ids = pack_rows(quot_row, quot_target, wide_size * quot_slots, -1).reshape(
        wide_size, quot_slots
    )
    rem_ids = pack_rows(rem_row, rem_target, narrow_size * rem_slots, -1).reshape(
        narrow_size, rem_slots
    )
    dequant = (quot_table.astype(jnp.float32) * quot_scale[:, None]).astype(jnp.bfloat16)
    grads = out_grad.astype(jnp.float32)
    fetched = jnp.take(
        rem_table,
        jnp.maximum(lax.all_to_all(rem_ids, "narrow", split_axis=0, concat_axis=0, tiled=True), 0),
        axis=0,
    )
    returned = lax.all_to_all(fetched, "narrow", split_axis=0, concat_axis=0, tiled=True)
    rem_tok = jnp.take(returned.reshape(-1, width), rem_target, axis=0)
    product = (grads * rem_tok.astype(jnp.float32)).astype(jnp.bfloat16)
    got_ids = lax.all_to_all(quot_ids, "wide", split_axis=0, concat_axis=0, tiled=True)
    got_prod = lax.all_to_all(
        pack_rows(product, quot_target, wide_size * quot_slots, jnp.bfloat16(0)).reshape(
            wide_size, quot_slots, width
        ),
        "wide",
        split_axis=0,
        concat_axis=0,
        tiled=True,
    )
    fetched = jnp.take(dequant, jnp.maximum(got_ids, 0), axis=0)
    quot_back = lax.all_to_all(fetched, "wide", split_axis=0, concat_axis=0, tiled=True)
    quot_rows = dequant.shape[0]
    selector = (jnp.arange(quot_rows, dtype=jnp.int32)[:, None] == got_ids.reshape(1, -1)).astype(
        jnp.bfloat16
    )
    partial_quot = jnp.dot(
        selector, got_prod.reshape(-1, width), preferred_element_type=jnp.float32
    )
    grad_quot = lax.psum(partial_quot, "narrow")
    quot_tok = jnp.take(quot_back.reshape(-1, width), quot_target, axis=0)
    prod_r = (grads * quot_tok.astype(jnp.float32)).astype(jnp.bfloat16)
    rem_prod = pack_rows(prod_r, rem_target, narrow_size * rem_slots, jnp.bfloat16(0)).reshape(
        narrow_size, rem_slots, width
    )
    recv_ids, recv_prod = (
        lax.all_to_all(rem_ids, "narrow", split_axis=0, concat_axis=0, tiled=True),
        lax.all_to_all(rem_prod, "narrow", split_axis=0, concat_axis=0, tiled=True),
    )
    flat_ids = recv_ids.reshape(-1)
    flat_prod = recv_prod.reshape(-1, width)
    rows_each = rem_table.shape[0] // wide_size
    local_rows = jnp.arange(lax.axis_size("wide") * rows_each, dtype=jnp.int32)
    picker = (local_rows[:, None] == flat_ids[None, :]).astype(jnp.bfloat16)
    grad_rem = lax.psum_scatter(
        jnp.dot(picker, flat_prod, preferred_element_type=jnp.float32),
        "wide",
        scatter_dimension=0,
        tiled=True,
    )
    return (grad_quot, grad_rem[None])


def solution(mesh):
    placed = (
        P(("wide", "narrow"), None),
        P(("wide", "narrow")),
        P(("wide", "narrow"), None),
        P(("wide", "narrow")),
        P(("wide", "narrow"), None),
        P("wide", None),
        P("wide"),
        P("narrow", None),
    )
    return jax.shard_map(
        on_device,
        mesh=mesh,
        in_specs=placed,
        out_specs=(P("wide", None), P("narrow", "wide", None)),
        check_vma=False,
    )
```

profile of v0, /device:TPU:6, one launch (start us, length us, event | category | flops | bytes accessed | tf_op | source)
XLA Modules:
  0.0 296.3 jit_solution(1333337250371145643)
XLA Ops:
  8.1 0.8 fusion.24
  8.9 1.1 reduce-window.16
  10.0 0.2 slice_reduce_fusion.1
  10.3 0.8 fusion.23
  11.1 0.7 and_reduce_fusion.1
  11.8 2.6 scatter_custom_fusion.1
  14.4 0.7 all_to_all.27
  15.0 7.1 %all-to-all-start.1 = ((s32[8,1,64]{2,1,0:T(1,128)}), s32[8,1,64]{2,1,0:T(1,128)S(1)}, u32[]{:S(2)}, u32[]{:S(2)}) async-start(s32[8,1,64]{2,1,0:T(1,128)} %all_to_all.27), calls=%async_computation.1 | async-start | bytes 8192 | tf_op jit(solution)/shard_map/all_to_all | solution.py:40
  22.1 0.7 fusion.21
  22.8 1.2 reduce-window.14
  24.0 5.7 %all-to-all-done.1 = s32[8,1,64]{2,1,0:T(1,128)S(1)} async-done(((s32[8,1,64]{2,1,0:T(1,128)}), s32[8,1,64]{2,1,0:T(1,128)S(1)}, u32[]{:S(2)}, u32[]{:S(2)}) %all-to-all-start.1) | async-done | bytes 2080 | tf_op jit(solution)/shard_map/all_to_all | solution.py:40
  29.8 0.1 reshape.134
  29.8 1.9 gather_fusion
  31.8 0.8 broadcast_select_fusion.1
  32.6 3.4 %all-to-all-start.2 = ((bf16[8,64,256]{2,1,0:T(8,128)(2,1)}), bf16[8,64,256]{2,1,0:T(8,128)(2,1)S(1)}, u32[]{:S(2)}, u32[]{:S(2)}) async-start(bf16[8,64,256]{2,1,0:T(8,128)(2,1)} %broadcast_select_fusion.1), calls=%async_computation.2 | async-start | bytes 524288 | tf_op jit(solution)/shard_map/all_to_all | solution.py:43
  36.1 0.2 slice_reduce_fusion
  36.3 0.8 fusion.17
  37.2 2.6 scatter_custom_fusion
  39.8 0.7 all_to_all.25
  40.5 6.2 %all-to-all-done.2 = bf16[8,64,256]{2,1,0:T(8,128)(2,1)S(1)} async-done(((bf16[8,64,256]{2,1,0:T(8,128)(2,1)}), bf16[8,64,256]{2,1,0:T(8,128)(2,1)S(1)}, u32[]{:S(2)}, u32[]{:S(2)}) %all-to-all-start.2) | async-done | bytes 262176 | tf_op jit(solution)/shard_map/all_to_all | solution.py:43
  46.7 14.0 %all-to-all-start = ((s32[64,1,16]{2,1,0:T(1,128)}), s32[64,1,16]{2,1,0:T(1,128)S(1)}, u32[]{:S(2)}, u32[]{:S(2)}) async-start(s32[64,1,16]{2,1,0:T(1,128)} %bitcast.5), calls=%async_computation | async-start | bytes 65536 | tf_op jit(solution)/shard_map/all_to_all | solution.py:46
  60.8 4.7 %scatter_custom_fusion.2 = bf16[1024,256]{1,0:T(8,128)(2,1)} fusion(s32[512]{0:T(512)S(1)} %bitcast.72, bf16[512,256]{1,0:T(8,128)(2,1)S(1)} %copy-done.1, bf16[]{:T(256)} %constant.76.clone.1, pred[512]{0:T(512)(128)(4,1)S(1)} %get-tuple-element.4, bf16[]{:T(256)} %constant.81.clone.1, bf16[512,256]{1,0:T(8,128)(2,1)S(1)} %bitcast.58, ...), kind=kCustom, calls=%fused_computation.21 | custom fusion | flops 655360 | bytes 1053188 | tf_op jit(solution)/shard_map/scatter | solution.py:17
  65.4 2.8 all-to-all-done
  68.2 7.7 %all-to-all-start.3 = ((bf16[64,16,256]{2,1,0:T(8,128)(2,1)}), bf16[64,16,256]{2,1,0:T(8,128)(2,1)}, u32[]{:S(2)}, u32[]{:S(2)}) async-start(bf16[64,16,256]{2,1,0:T(8,128)(2,1)} %bitcast.16), calls=%async_computation.3 | async-start | bytes 1048576 | tf_op jit(solution)/shard_map/all_to_all | solution.py:47
  76.0 0.2 multiply_convert_fusion
  76.2 0.1 copy.16
  76.2 0.1 copy.18
  76.3 0.1 reshape.150
  76.4 0.1 copy.17
  76.5 3.9 %gather_fusion.1 = bf16[1024,256]{1,0:T(8,128)(2,1)S(1)} fusion(bf16[1024,256]{1,0:T(8,128)(2,1)S(1)} %multiply_convert_fusion, s32[1024]{0:T(1024)S(1)} %broadcast_clamp_fusion), kind=kCustom, calls=%fused_computation.2 | custom fusion | bytes 1052672 | tf_op jit(solution)/shard_map/jit(_take)/gather | solution.py:56
  80.5 1.0 broadcast_select_fusion
  81.5 11.1 %all-to-all-done.3 = bf16[64,16,256]{2,1,0:T(8,128)(2,1)} async-done(((bf16[64,16,256]{2,1,0:T(8,128)(2,1)}), bf16[64,16,256]{2,1,0:T(8,128)(2,1)}, u32[]{:S(2)}, u32[]{:S(2)}) %all-to-all-start.3) | async-done | bytes 524320 | tf_op jit(solution)/shard_map/all_to_all | solution.py:47
  92.6 6.9 %all-to-all-start.4 = ((bf16[64,16,256]{2,1,0:T(8,128)(2,1)}), bf16[64,16,256]{2,1,0:T(8,128)(2,1)S(1)}, u32[]{:S(2)}, u32[]{:S(2)}) async-start(bf16[64,16,256]{2,1,0:T(8,128)(2,1)} %broadcast_select_fusion), calls=%async_computation.4 | async-start | bytes 1048576 | tf_op jit(solution)/shard_map/all_to_all | solution.py:57
  99.5 0.2 all-reduce.2.cloned.1.call-start
  99.7 0.5 broadcast.143
  100.2 0.7 reduce.14
  100.9 0.1 eq.89
  101.0 2.8 fusion.2
  103.9 12.3 %all-to-all-done.4 = bf16[64,16,256]{2,1,0:T(8,128)(2,1)S(1)} async-done(((bf16[64,16,256]{2,1,0:T(8,128)(2,1)}), bf16[64,16,256]{2,1,0:T(8,128)(2,1)S(1)}, u32[]{:S(2)}, u32[]{:S(2)}) %all-to-all-start.4) | async-done | bytes 524320 | tf_op jit(solution)/shard_map/all_to_all | solution.py:57
  116.2 4.5 %scatter_custom_fusion.3 = bf16[512,256]{1,0:T(8,128)(2,1)} fusion(s32[512]{0:T(512)S(1)} %bitcast.70, bf16[512,256]{1,0:T(8,128)(2,1)S(1)} %copy-done.1, pred[512]{0:T(512)(128)(4,1)S(1)} %get-tuple-element.2, bf16[]{:T(256)} %constant.76.clone.1, bf16[]{:T(256)} %constant.81.clone.1, bf16[1024,256]{1,0:T(8,128)(2,1)S(1)} %bitcast.57, ...), kind=kCustom, calls=%fused_computation.20 | custom fusion | flops 655360 | bytes 1053188 | tf_op jit(solution)/shard_map/scatter | solution.py:17
  120.7 3.4 %all-to-all-start.5 = ((bf16[8,64,256]{2,1,0:T(8,128)(2,1)}), bf16[8,64,256]{2,1,0:T(8,128)(2,1)S(1)}, u32[]{:S(2)}, u32[]{:S(2)}) async-start(bf16[8,64,256]{2,1,0:T(8,128)(2,1)} %bitcast.21), calls=%async_computation.5 | async-start | bytes 524288 | tf_op jit(solution)/shard_map/all_to_all | solution.py:73
  124.2 0.7 reduce.15
  124.8 0.1 eq.101
  124.9 13.6 %all-to-all-done.5 = bf16[8,64,256]{2,1,0:T(8,128)(2,1)S(1)} async-done(((bf16[8,64,256]{2,1,0:T(8,128)(2,1)}), bf16[8,64,256]{2,1,0:T(8,128)(2,1)S(1)}, u32[]{:S(2)}, u32[]{:S(2)}) %all-to-all-start.5) | async-done | bytes 262176 | tf_op jit(solution)/shard_map/all_to_all | solution.py:73
  138.5 3.4 %fusion = f32[4096,256]{1,0:T(8,128)} fusion(bf16[512,256]{1,0:T(8,128)(2,1)S(1)} %bitcast.60, s32[512]{0:T(512)S(1)} %eq.101), kind=kOutput, calls=%fused_computation.9 | convolution fusion | flops 1075838976 | bytes 4458496 | tf_op jit(solution)/shard_map/dot_general | solution.py:81
  141.9 43.0 %all-reduce.2.cloned.1.call-done = f32[1024,256]{1,0:T(8,128)} async-done(((f32[1024,256]{1,0:T(8,128)}), f32[1024,256]{1,0:T(8,128)}) %all-reduce.2.cloned.1.call-update) | async-done | bytes 1048592 | tf_op jit(solution)/shard_map/psum | solution.py:65
  184.9 101.7 %reduce-scatter.2.cloned.1.call-done = f32[64,256]{1,0:T(8,128)} async-done(((f32[4096,256]{1,0:T(8,128)}), f32[64,256]{1,0:T(8,128)}) %reduce-scatter.2.cloned.1.call-update) | async-done | bytes 65552 | tf_op jit(solution)/shard_map/reduce_scatter | solution.py:80
  286.6 2.3 copy.22
  (26 shorter events, 0.3 us)
Async XLA Ops:
  8.0 21.8 %copy-start = (bf16[4096,256]{1,0:T(8,128)(2,1)S(1)}, bf16[4096,256]{1,0:T(8,128)(2,1)}, u32[]{:S(2)}) copy-start(bf16[4096,256]{1,0:T(8,128)(2,1)} %param.15) | copy-start | bytes 6291460
  8.0 29.1 %copy-start.3 = (s32[512,1]{0,1:T(1,128)S(1)}, s32[512,1]{0,1:T(1,128)}, u32[]{:S(2)}) copy-start(s32[512,1]{0,1:T(1,128)} %param.8) | copy-start | bytes 6148
  8.0 52.7 %copy-start.1 = (bf16[512,256]{1,0:T(8,128)(2,1)S(1)}, bf16[512,256]{1,0:T(8,128)(2,1)}, u32[]{:S(2)}) copy-start(bf16[512,256]{1,0:T(8,128)(2,1)} %param.12) | copy-start | bytes 786436
  8.0 67.9 %copy-start.2 = (bf16[1024,256]{1,0:T(8,128)(2,1)S(1)}, bf16[1024,256]{1,0:T(8,128)(2,1)}, u32[]{:S(2)}) copy-start(bf16[1024,256]{1,0:T(8,128)(2,1)} %param.13) | copy-start | bytes 1572868
  8.0 67.9 %copy-start.4 = (f32[1024]{0:T(1024)S(1)}, f32[1024]{0:T(1024)}, u32[]{:S(2)}) copy-start(f32[1024]{0:T(1024)} %param.14) | copy-start | bytes 12292
  15.0 14.7 %all-to-all-start.1 = ((s32[8,1,64]{2,1,0:T(1,128)}), s32[8,1,64]{2,1,0:T(1,128)S(1)}, u32[]{:S(2)}, u32[]{:S(2)}) async-start(s32[8,1,64]{2,1,0:T(1,128)} %all_to_all.27), calls=%async_computation.1 | async-start | bytes 8192 | tf_op jit(solution)/shard_map/all_to_all | solution.py:40
  32.6 14.1 %all-to-all-start.2 = ((bf16[8,64,256]{2,1,0:T(8,128)(2,1)}), bf16[8,64,256]{2,1,0:T(8,128)(2,1)S(1)}, u32[]{:S(2)}, u32[]{:S(2)}) async-start(bf16[8,64,256]{2,1,0:T(8,128)(2,1)} %broadcast_select_fusion.1), calls=%async_computation.2 | async-start | bytes 524288 | tf_op jit(solution)/shard_map/all_to_all | solution.py:43
  46.7 21.5 %all-to-all-start = ((s32[64,1,16]{2,1,0:T(1,128)}), s32[64,1,16]{2,1,0:T(1,128)S(1)}, u32[]{:S(2)}, u32[]{:S(2)}) async-start(s32[64,1,16]{2,1,0:T(1,128)} %bitcast.5), calls=%async_computation | async-start | bytes 65536 | tf_op jit(solution)/shard_map/all_to_all | solution.py:46
  68.2 24.3 %all-to-all-start.3 = ((bf16[64,16,256]{2,1,0:T(8,128)(2,1)}), bf16[64,16,256]{2,1,0:T(8,128)(2,1)}, u32[]{:S(2)}, u32[]{:S(2)}) async-start(bf16[64,16,256]{2,1,0:T(8,128)(2,1)} %bitcast.16), calls=%async_computation.3 | async-start | bytes 1048576 | tf_op jit(solution)/shard_map/all_to_all | solution.py:47
  92.6 23.6 %all-to-all-start.4 = ((bf16[64,16,256]{2,1,0:T(8,128)(2,1)}), bf16[64,16,256]{2,1,0:T(8,128)(2,1)S(1)}, u32[]{:S(2)}, u32[]{:S(2)}) async-start(bf16[64,16,256]{2,1,0:T(8,128)(2,1)} %broadcast_select_fusion), calls=%async_computation.4 | async-start | bytes 1048576 | tf_op jit(solution)/shard_map/all_to_all | solution.py:57
  99.5 85.4 %all-reduce.2.cloned.1.call-start = ((), (), s32[]{:S(2)}) async-start(), calls=%async_computation.7 | async-start | bytes 2097152 | tf_op jit(solution)/shard_map/psum | solution.py:65
  120.7 17.8 %all-to-all-start.5 = ((bf16[8,64,256]{2,1,0:T(8,128)(2,1)}), bf16[8,64,256]{2,1,0:T(8,128)(2,1)S(1)}, u32[]{:S(2)}, u32[]{:S(2)}) async-start(bf16[8,64,256]{2,1,0:T(8,128)(2,1)} %bitcast.21), calls=%async_computation.5 | async-start | bytes 524288 | tf_op jit(solution)/shard_map/all_to_all | solution.py:73
  124.1 162.5 %reduce-scatter.2.cloned.1.call-start = ((), (), s32[]{:S(2)}) async-start(), calls=%async_computation.8 | async-start | bytes 4259840 | tf_op jit(solution)/shard_map/reduce_scatter | solution.py:80
Sparse Core Ops, SparseCore 0:
  104.0 80.8 all-reduce.1
Sparse Core Ops, SparseCore 1:
  142.0 144.5 reduce-scatter.1
where the time goes:
time: 298 us; the launch traced here: 296 us
  waiting for transfers between devices  196 us (66%)
  starting transfers between devices  42.8 us (14%)
  other arithmetic  18.9 us (6%)
  local copies, waits for them, and re-layouts  16.3 us (5%)
  between operations  15.7 us (5%)
  matrix products  6.16 us (2%)
    reduce_scatter x1, waiting for transfers between devices, on_device(): lax.psum_scatter(jnp.dot(picker, flat_prod, preferred_element_type=jnp.fl...  102 us
    psum x1, waiting for transfers between devices, on_device(): grad_quot = lax.psum(partial_quot, 'narrow')  43 us
    all_to_all x1, starting transfers between devices, on_device(): lax.all_to_all(quot_ids, 'wide', split_axis=0, concat_axis=0, tiled=True)  14 us
    all_to_all x1, waiting for transfers between devices, on_device(): lax.all_to_all(rem_prod, 'narrow', split_axis=0, concat_axis=0, tiled=True)  13.6 us
    all_to_all x1, waiting for transfers between devices, on_device(): lax.all_to_all(fetched, 'wide', split_axis=0, concat_axis=0, tiled=True)  12.3 us
    all_to_all x1, waiting for transfers between devices, on_device(): lax.all_to_all(pack_rows(product, quot_target, wide_size * quot_slots, jn...  11.1 us
    scatter x2, other arithmetic, pack_rows(): jnp.full(full_shape, filler, values.dtype).at[target]  9.17 us
    all_to_all x1, starting transfers between devices, on_device(): lax.all_to_all(pack_rows(product, quot_target, wide_size * quot_slots, jn...  7.7 us
  transfers between devices with their start and end apart: 8, of which 8 were waited for; matrix products, arithmetic and copies ran while one was open for 10% of the time, Pallas kernels for 0%

commit v1 on v0

v1 whole, which is shorter than its diff:
```python
import jax
import jax.numpy as jnp
from jax import lax
from jax.sharding import PartitionSpec as P

BLOCK_CAP = 2


def earlier_equal(keys):
    size = keys.shape[-1]
    before = jnp.arange(size)[None, :] < jnp.arange(size)[:, None]
    same = keys[..., :, None] == keys[..., None, :]
    return jnp.sum((same & before).astype(jnp.int32), axis=-1)


def slot_mask(slots, target):
    return jnp.arange(slots, dtype=jnp.int32)[:, None] == target[None, :]


def pack_ints(mask, values):
    return jnp.max(jnp.where(mask, values[None, :], -1), axis=1)


def select_rows(mask, values, contract=1):
    return lax.dot_general(
        mask.astype(jnp.bfloat16),
        values,
        (((contract,), (0,)), ((), ())),
        preferred_element_type=jnp.float32,
    )


def exchange(value, axis):
    return lax.all_to_all(value, axis, split_axis=0, concat_axis=0, tiled=True)


def on_device(
    quot_owner, quot_row, rem_owner, rem_row, out_grad, quot_table, quot_scale, rem_table
):
    wide_size = lax.axis_size("wide")
    narrow_size = lax.axis_size("narrow")
    tokens, width = out_grad.shape
    quot_slots = 2 * tokens // wide_size
    rem_slots = tokens // narrow_size
    block_slots = BLOCK_CAP * narrow_size
    quot_rows = quot_table.shape[0]
    rows_each = rem_table.shape[0] // wide_size
    quot_owner, rem_owner = quot_owner[:, 0], rem_owner[:, 0]

    rem_target = rem_owner * rem_slots + earlier_equal(rem_owner)
    rem_mask = slot_mask(tokens, rem_target)
    rem_ids = exchange(pack_ints(rem_mask, rem_row).reshape(narrow_size, rem_slots), "narrow")

    quot_target = quot_owner * quot_slots + earlier_equal(quot_owner)
    quot_mask = slot_mask(wide_size * quot_slots, quot_target)
    got_ids = exchange(
        pack_ints(quot_mask, quot_row).reshape(wide_size, quot_slots), "wide"
    ).reshape(-1)

    grads = out_grad.astype(jnp.float32)
    fetched = rem_table.at[rem_ids].get(mode="promise_in_bounds")
    returned = exchange(fetched, "narrow").reshape(-1, width)

    dequant = (quot_table.astype(jnp.float32) * quot_scale[:, None]).astype(jnp.bfloat16)
    quot_pick = slot_mask(quot_rows, got_ids)
    quot_fetched = select_rows(quot_pick, dequant, 0).astype(jnp.bfloat16)
    quot_back = exchange(quot_fetched.reshape(wide_size, quot_slots, width), "wide")

    rem_tok = select_rows(rem_mask, returned, 0)
    product = (grads * rem_tok).astype(jnp.bfloat16)
    got_prod = exchange(
        select_rows(quot_mask, product)
        .astype(jnp.bfloat16)
        .reshape(wide_size, quot_slots, width),
        "wide",
    ).reshape(-1, width)

    quot_tok = select_rows(quot_mask, quot_back.reshape(-1, width), 0)
    prod_r = (grads * quot_tok).astype(jnp.bfloat16)
    rem_prod = exchange(
        select_rows(rem_mask, prod_r)
        .astype(jnp.bfloat16)
        .reshape(narrow_size, rem_slots, width),
        "narrow",
    ).reshape(-1, width)

    block = rem_ids // rows_each
    peers = jnp.arange(narrow_size, dtype=jnp.int32)[:, None]
    block_target = block * block_slots + peers * BLOCK_CAP + earlier_equal(block)
    block_mask = slot_mask(wide_size * block_slots, block_target.reshape(-1))
    block_ids = exchange(
        pack_ints(block_mask, (rem_ids % rows_each).reshape(-1)).reshape(
            wide_size, block_slots
        ),
        "wide",
    ).reshape(-1)
    block_prod = exchange(
        select_rows(block_mask, rem_prod)
        .astype(jnp.bfloat16)
        .reshape(wide_size, block_slots, width),
        "wide",
    ).reshape(-1, width)

    partial = select_rows(quot_pick, got_prod).astype(jnp.bfloat16)
    parts = exchange(partial.reshape(narrow_size, -1, width), "narrow")
    share = jnp.sum(parts.astype(jnp.float32), axis=0).astype(jnp.bfloat16)
    copies = jnp.broadcast_to(share[None], (narrow_size,) + share.shape)
    grad_quot = exchange(copies, "narrow").reshape(-1, width).astype(jnp.float32)

    grad_rem = select_rows(slot_mask(rows_each, block_ids), block_prod)
    return (grad_quot, grad_rem[None])


def solution(mesh):
    placed = (
        P(("wide", "narrow"), None),
        P(("wide", "narrow")),
        P(("wide", "narrow"), None),
        P(("wide", "narrow")),
        P(("wide", "narrow"), None),
        P("wide", None),
        P("wide"),
        P("narrow", None),
    )
    return jax.shard_map(
        on_device,
        mesh=mesh,
        in_specs=placed,
        out_specs=(P("wide", None), P("narrow", "wide", None)),
        check_vma=False,
    )
```

time: 298 us -> 203 us (0.68)
  waiting for transfers between devices: 196 us -> 112 us
  starting transfers between devices: 42.8 us -> 61 us
  between operations: 15.7 us -> 0.84 us
  local copies, waits for them, and re-layouts: 16.3 us -> 6.59 us
  other arithmetic: 18.9 us -> 9.54 us
  matrix products: 6.16 us -> 11.3 us
    reduce_scatter x1 -> x0, waiting for transfers between devices: 102 us -> none  [on_device(): lax.psum_scatter(jnp.dot(picker, flat_prod, preferred_element_type=jnp.fl...]
    all_to_all x6 -> x10, waiting for transfers between devices: 51.7 us -> 112 us  [exchange(): return lax.all_to_all(value, axis, split_axis=0, concat_axis=0, tiled=True)]
    psum x1 -> x0, waiting for transfers between devices: 43 us -> none  [on_device(): grad_quot = lax.psum(partial_quot, 'narrow')]
    all_to_all x6 -> x10, starting transfers between devices: 42.5 us -> 61 us  [exchange(): return lax.all_to_all(value, axis, split_axis=0, concat_axis=0, tiled=True)]
    scatter x2 -> x0, other arithmetic: 9.17 us -> none  [pack_rows(): jnp.full(full_shape, filler, values.dtype).at[target]]
    scatter x2 -> x0, local copies, waits for them, and re-layouts: 5.19 us -> none  [pack_rows(): jnp.full(full_shape, filler, values.dtype).at[target]]
    dot_general x2 -> x6, matrix products: 6.16 us -> 11.3 us  [select_rows(): lax.dot_general(mask.astype(jnp.bfloat16), values, (((contract,), (0,)),...]
    gather x2 -> x1, local copies, waits for them, and re-layouts: 5.89 us -> 2.58 us  [on_device(): fetched = rem_table.at[rem_ids].get(mode='promise_in_bounds')]
  transfers between devices with their start and end apart: 8 -> 10, of which waited for: 8 -> 10; matrix products, arithmetic and copies ran while one was open for 10% -> 10% of each run, Pallas kernels for 0% -> 0%
where the time goes in v1:
time: 203 us; the launch traced here: 201 us
  waiting for transfers between devices  112 us (55%)
  starting transfers between devices  61 us (30%)
  matrix products  11.3 us (6%)
  other arithmetic  9.54 us (5%)
  local copies, waits for them, and re-layouts  6.59 us (3%)
    all_to_all x10, waiting for transfers between devices, exchange(): return lax.all_to_all(value, axis, split_axis=0, concat_axis=0, tiled=True)  112 us
    all_to_all x10, starting transfers between devices, exchange(): return lax.all_to_all(value, axis, split_axis=0, concat_axis=0, tiled=True)  61 us
    dot_general x6, matrix products, select_rows(): lax.dot_general(mask.astype(jnp.bfloat16), values, (((contract,), (0,)),...  11.3 us
  transfers between devices with their start and end apart: 10, of which 10 were waited for; matrix products, arithmetic and copies ran while one was open for 10% of the time, Pallas kernels for 0%

profile of v1, /device:TPU:6, one launch (start us, length us, event | category | flops | bytes accessed | tf_op | source)
XLA Modules:
  0.0 201.2 jit_solution(6804341445155916537)
XLA Ops:
  0.7 1.1 convert_reduce_fusion
  1.8 0.7 multiply_add_fusion
  2.4 0.9 select_reduce_fusion.2
  3.3 0.7 all_to_all.47
  4.0 7.1 %all-to-all-start.1 = ((s32[8,1,64]{2,1,0:T(1,128)}), s32[8,1,64]{2,1,0:T(1,128)S(1)}, u32[]{:S(2)}, u32[]{:S(2)}) async-start(s32[8,1,64]{2,1,0:T(1,128)} %all_to_all.47), calls=%async_computation.1 | async-start | bytes 8192 | tf_op jit(solution)/shard_map/all_to_all | solution.py:34
  11.1 1.0 convert_reduce_fusion.1
  12.1 0.7 multiply_add_fusion.1
  12.8 1.0 select_reduce_fusion.1
  13.9 0.1 add.73
  14.0 0.7 all_to_all.45
  14.7 4.0 %all-to-all-done.1 = s32[8,1,64]{2,1,0:T(1,128)S(1)} async-done(((s32[8,1,64]{2,1,0:T(1,128)}), s32[8,1,64]{2,1,0:T(1,128)S(1)}, u32[]{:S(2)}, u32[]{:S(2)}) %all-to-all-start.1) | async-done | bytes 2080 | tf_op jit(solution)/shard_map/all_to_all | solution.py:34
  18.7 14.0 %all-to-all-start = ((s32[64,1,16]{2,1,0:T(1,128)}), s32[64,1,16]{2,1,0:T(1,128)S(1)}, u32[]{:S(2)}, u32[]{:S(2)}) async-start(s32[64,1,16]{2,1,0:T(1,128)} %bitcast.1), calls=%async_computation | async-start | bytes 65536 | tf_op jit(solution)/shard_map/all_to_all | solution.py:34
  32.8 0.6 broadcast.163
  33.4 0.7 fusion.33
  34.1 0.1 all_to_all.54
  34.2 0.3 convert_reduce_fusion.2
  34.5 0.1 reduce_sum.45
  34.6 0.4 select_reduce_fusion
  35.0 0.7 all_to_all.56
  35.7 4.5 %all-to-all-done = s32[64,1,16]{2,1,0:T(1,128)S(1)} async-done(((s32[64,1,16]{2,1,0:T(1,128)}), s32[64,1,16]{2,1,0:T(1,128)S(1)}, u32[]{:S(2)}, u32[]{:S(2)}) %all-to-all-start) | async-done | bytes 4128 | tf_op jit(solution)/shard_map/all_to_all | solution.py:34
  40.3 6.5 %all-to-all-start.6 = ((s32[64,1,16]{2,1,0:T(1,128)}), s32[64,1,16]{2,1,0:T(1,128)S(1)}, u32[]{:S(2)}, u32[]{:S(2)}) async-start(s32[64,1,16]{2,1,0:T(1,128)} %bitcast.12), calls=%async_computation.6 | async-start | bytes 65536 | tf_op jit(solution)/shard_map/all_to_all | solution.py:34
  46.8 2.6 %gather_fusion = bf16[512,256]{1,0:T(8,128)(2,1)} fusion(bf16[4096,256]{1,0:T(8,128)(2,1)S(1)} %copy-done, s32[1024]{0:T(1024)S(1)} %pad_clamp_fusion), kind=kCustom, calls=%fused_computation | custom fusion | bytes 526336 | tf_op jit(solution)/shard_map/gather | solution.py:61
  49.4 5.0 %all-to-all-done.6 = s32[64,1,16]{2,1,0:T(1,128)S(1)} async-done(((s32[64,1,16]{2,1,0:T(1,128)}), s32[64,1,16]{2,1,0:T(1,128)S(1)}, u32[]{:S(2)}, u32[]{:S(2)}) %all-to-all-start.6) | async-done | bytes 4128 | tf_op jit(solution)/shard_map/all_to_all | solution.py:34
  54.4 3.4 %all-to-all-start.2 = ((bf16[8,64,256]{2,1,0:T(8,128)(2,1)}), bf16[8,64,256]{2,1,0:T(8,128)(2,1)S(1)}, u32[]{:S(2)}, u32[]{:S(2)}) async-start(bf16[8,64,256]{2,1,0:T(8,128)(2,1)} %bitcast.4), calls=%async_computation.2 | async-start | bytes 524288 | tf_op jit(solution)/shard_map/all_to_all | solution.py:34
  57.8 0.8 reduce.10
  58.6 0.1 eq.117
  58.7 2.2 %fusion.10 = bf16[1024,256]{1,0:T(8,128)(2,1)} fusion(s32[1024]{0:T(1024)S(1)} %eq.117, bf16[1024,256]{1,0:T(8,128)(2,1)S(1)} %copy-done.1, f32[1024]{0:T(1024)S(1)} %copy-done.2), kind=kOutput, calls=%fused_computation.16 | convolution fusion | flops 538968064 | bytes 1056768 | tf_op jit(solution)/shard_map/dot_general | solution.py:25
  60.9 9.0 %all-to-all-done.2 = bf16[8,64,256]{2,1,0:T(8,128)(2,1)S(1)} async-done(((bf16[8,64,256]{2,1,0:T(8,128)(2,1)}), bf16[8,64,256]{2,1,0:T(8,128)(2,1)S(1)}, u32[]{:S(2)}, u32[]{:S(2)}) %all-to-all-start.2) | async-done | bytes 262176 | tf_op jit(solution)/shard_map/all_to_all | solution.py:34
  69.9 6.5 %all-to-all-start.7 = ((bf16[64,16,256]{2,1,0:T(8,128)(2,1)}), bf16[64,16,256]{2,1,0:T(8,128)(2,1)S(1)}, u32[]{:S(2)}, u32[]{:S(2)}) async-start(bf16[64,16,256]{2,1,0:T(8,128)(2,1)} %bitcast.13), calls=%async_computation.7 | async-start | bytes 1048576 | tf_op jit(solution)/shard_map/all_to_all | solution.py:34
  76.4 2.7 %fusion.7 = bf16[1024,256]{1,0:T(8,128)(2,1)} fusion(bf16[512,256]{1,0:T(8,128)(2,1)S(1)} %bitcast.36, s32[512]{0:T(512)S(1)} %multiply_add_fusion.1, bf16[512,256]{1,0:T(8,128)(2,1)} %param.12, s32[512]{0:T(512)S(1)} %multiply_add_fusion), kind=kOutput, calls=%fused_computation.13 | convolution fusion | flops 404094976 | bytes 1052672 | tf_op jit(solution)/shard_map/dot_general | solution.py:25
  79.1 14.0 %all-to-all-done.7 = bf16[64,16,256]{2,1,0:T(8,128)(2,1)S(1)} async-done(((bf16[64,16,256]{2,1,0:T(8,128)(2,1)}), bf16[64,16,256]{2,1,0:T(8,128)(2,1)S(1)}, u32[]{:S(2)}, u32[]{:S(2)}) %all-to-all-start.7) | async-done | bytes 524320 | tf_op jit(solution)/shard_map/all_to_all | solution.py:34
  93.1 6.9 %all-to-all-start.3 = ((bf16[64,16,256]{2,1,0:T(8,128)(2,1)}), bf16[64,16,256]{2,1,0:T(8,128)(2,1)S(1)}, u32[]{:S(2)}, u32[]{:S(2)}) async-start(bf16[64,16,256]{2,1,0:T(8,128)(2,1)} %bitcast.33), calls=%async_computation.3 | async-start | bytes 1048576 | tf_op jit(solution)/shard_map/all_to_all | solution.py:34
  100.0 2.7 %convolution_convert_fusion = bf16[512,256]{1,0:T(8,128)(2,1)} fusion(bf16[1024,256]{1,0:T(8,128)(2,1)S(1)} %bitcast.32, s32[512]{0:T(512)S(1)} %multiply_add_fusion.1, bf16[512,256]{1,0:T(8,128)(2,1)} %param.12, s32[512]{0:T(512)S(1)} %multiply_add_fusion), kind=kOutput, calls=%fused_computation.19 | convolution fusion | flops 403963904 | bytes 1052672 | tf_op jit(solution)/shard_map/dot_general | solution.py:25
  102.7 14.0 %all-to-all-done.3 = bf16[64,16,256]{2,1,0:T(8,128)(2,1)S(1)} async-done(((bf16[64,16,256]{2,1,0:T(8,128)(2,1)}), bf16[64,16,256]{2,1,0:T(8,128)(2,1)S(1)}, u32[]{:S(2)}, u32[]{:S(2)}) %all-to-all-start.3) | async-done | bytes 524320 | tf_op jit(solution)/shard_map/all_to_all | solution.py:34
  116.8 3.4 %all-to-all-start.8 = ((bf16[8,64,256]{2,1,0:T(8,128)(2,1)}), bf16[8,64,256]{2,1,0:T(8,128)(2,1)S(1)}, u32[]{:S(2)}, u32[]{:S(2)}) async-start(bf16[8,64,256]{2,1,0:T(8,128)(2,1)} %bitcast.38), calls=%async_computation.8 | async-start | bytes 524288 | tf_op jit(solution)/shard_map/all_to_all | solution.py:34
  120.2 1.6 fusion.9
  121.8 11.2 %all-to-all-done.8 = bf16[8,64,256]{2,1,0:T(8,128)(2,1)S(1)} async-done(((bf16[8,64,256]{2,1,0:T(8,128)(2,1)}), bf16[8,64,256]{2,1,0:T(8,128)(2,1)S(1)}, u32[]{:S(2)}, u32[]{:S(2)}) %all-to-all-start.8) | async-done | bytes 262176 | tf_op jit(solution)/shard_map/all_to_all | solution.py:34
  133.0 3.5 %all-to-all-start.4 = ((bf16[8,128,256]{2,1,0:T(8,128)(2,1)}), bf16[8,128,256]{2,1,0:T(8,128)(2,1)S(1)}, u32[]{:S(2)}, u32[]{:S(2)}) async-start(bf16[8,128,256]{2,1,0:T(8,128)(2,1)} %bitcast.34), calls=%async_computation.4 | async-start | bytes 1048576 | tf_op jit(solution)/shard_map/all_to_all | solution.py:34
  136.5 1.3 fusion.8
  137.8 16.7 %all-to-all-done.4 = bf16[8,128,256]{2,1,0:T(8,128)(2,1)S(1)} async-done(((bf16[8,128,256]{2,1,0:T(8,128)(2,1)}), bf16[8,128,256]{2,1,0:T(8,128)(2,1)S(1)}, u32[]{:S(2)}, u32[]{:S(2)}) %all-to-all-start.4) | async-done | bytes 524320 | tf_op jit(solution)/shard_map/all_to_all | solution.py:34
  154.5 6.1 %all-to-all-start.9 = ((bf16[64,16,256]{2,1,0:T(8,128)(2,1)}), bf16[64,16,256]{2,1,0:T(8,128)(2,1)S(1)}, u32[]{:S(2)}, u32[]{:S(2)}) async-start(bf16[64,16,256]{2,1,0:T(8,128)(2,1)} %bitcast.35), calls=%async_computation.9 | async-start | bytes 1048576 | tf_op jit(solution)/shard_map/all_to_all | solution.py:34
  160.6 16.6 %all-to-all-done.9 = bf16[64,16,256]{2,1,0:T(8,128)(2,1)S(1)} async-done(((bf16[64,16,256]{2,1,0:T(8,128)(2,1)}), bf16[64,16,256]{2,1,0:T(8,128)(2,1)S(1)}, u32[]{:S(2)}, u32[]{:S(2)}) %all-to-all-start.9) | async-done | bytes 524320 | tf_op jit(solution)/shard_map/all_to_all | solution.py:34
  177.3 0.8 broadcast_in_dim.38
  178.1 3.5 %all-to-all-start.5 = ((bf16[8,128,256]{2,1,0:T(8,128)(2,1)}), bf16[8,128,256]{2,1,0:T(8,128)(2,1)S(1)}, u32[]{:S(2)}, u32[]{:S(2)}) async-start(bf16[8,128,256]{2,1,0:T(8,128)(2,1)} %broadcast_in_dim.38), calls=%async_computation.5 | async-start | bytes 1048576 | tf_op jit(solution)/shard_map/all_to_all | solution.py:34
  181.6 0.8 reduce.12
  182.5 0.8 convolution_bitcast_fusion
  183.3 16.8 %all-to-all-done.5 = bf16[8,128,256]{2,1,0:T(8,128)(2,1)S(1)} async-done(((bf16[8,128,256]{2,1,0:T(8,128)(2,1)}), bf16[8,128,256]{2,1,0:T(8,128)(2,1)S(1)}, u32[]{:S(2)}, u32[]{:S(2)}) %all-to-all-start.5) | async-done | bytes 524320 | tf_op jit(solution)/shard_map/all_to_all | solution.py:34
  200.1 1.1 bitcast_convert_fusion
  (16 shorter events, 0.4 us)
Async XLA Ops:
  0.6 46.2 %copy-start = (bf16[4096,256]{1,0:T(8,128)(2,1)S(1)}, bf16[4096,256]{1,0:T(8,128)(2,1)}, u32[]{:S(2)}) copy-start(bf16[4096,256]{1,0:T(8,128)(2,1)} %param.15) | copy-start | bytes 6291460
  0.6 58.0 %copy-start.2 = (f32[1024]{0:T(1024)S(1)}, f32[1024]{0:T(1024)}, u32[]{:S(2)}) copy-start(f32[1024]{0:T(1024)} %param.14) | copy-start | bytes 12292
  0.7 58.0 %copy-start.1 = (bf16[1024,256]{1,0:T(8,128)(2,1)S(1)}, bf16[1024,256]{1,0:T(8,128)(2,1)}, u32[]{:S(2)}) copy-start(bf16[1024,256]{1,0:T(8,128)(2,1)} %param.13) | copy-start | bytes 1572868
  4.0 14.7 %all-to-all-start.1 = ((s32[8,1,64]{2,1,0:T(1,128)}), s32[8,1,64]{2,1,0:T(1,128)S(1)}, u32[]{:S(2)}, u32[]{:S(2)}) async-start(s32[8,1,64]{2,1,0:T(1,128)} %all_to_all.47), calls=%async_computation.1 | async-start | bytes 8192 | tf_op jit(solution)/shard_map/all_to_all | solution.py:34
  18.7 21.5 %all-to-all-start = ((s32[64,1,16]{2,1,0:T(1,128)}), s32[64,1,16]{2,1,0:T(1,128)S(1)}, u32[]{:S(2)}, u32[]{:S(2)}) async-start(s32[64,1,16]{2,1,0:T(1,128)} %bitcast.1), calls=%async_computation | async-start | bytes 65536 | tf_op jit(solution)/shard_map/all_to_all | solution.py:34
  40.3 14.1 %all-to-all-start.6 = ((s32[64,1,16]{2,1,0:T(1,128)}), s32[64,1,16]{2,1,0:T(1,128)S(1)}, u32[]{:S(2)}, u32[]{:S(2)}) async-start(s32[64,1,16]{2,1,0:T(1,128)} %bitcast.12), calls=%async_computation.6 | async-start | bytes 65536 | tf_op jit(solution)/shard_map/all_to_all | solution.py:34
  54.4 15.5 %all-to-all-start.2 = ((bf16[8,64,256]{2,1,0:T(8,128)(2,1)}), bf16[8,64,256]{2,1,0:T(8,128)(2,1)S(1)}, u32[]{:S(2)}, u32[]{:S(2)}) async-start(bf16[8,64,256]{2,1,0:T(8,128)(2,1)} %bitcast.4), calls=%async_computation.2 | async-start | bytes 524288 | tf_op jit(solution)/shard_map/all_to_all | solution.py:34
  69.9 23.3 %all-to-all-start.7 = ((bf16[64,16,256]{2,1,0:T(8,128)(2,1)}), bf16[64,16,256]{2,1,0:T(8,128)(2,1)S(1)}, u32[]{:S(2)}, u32[]{:S(2)}) async-start(bf16[64,16,256]{2,1,0:T(8,128)(2,1)} %bitcast.13), calls=%async_computation.7 | async-start | bytes 1048576 | tf_op jit(solution)/shard_map/all_to_all | solution.py:34
  93.1 23.6 %all-to-all-start.3 = ((bf16[64,16,256]{2,1,0:T(8,128)(2,1)}), bf16[64,16,256]{2,1,0:T(8,128)(2,1)S(1)}, u32[]{:S(2)}, u32[]{:S(2)}) async-start(bf16[64,16,256]{2,1,0:T(8,128)(2,1)} %bitcast.33), calls=%async_computation.3 | async-start | bytes 1048576 | tf_op jit(solution)/shard_map/all_to_all | solution.py:34
  116.8 16.3 %all-to-all-start.8 = ((bf16[8,64,256]{2,1,0:T(8,128)(2,1)}), bf16[8,64,256]{2,1,0:T(8,128)(2,1)S(1)}, u32[]{:S(2)}, u32[]{:S(2)}) async-start(bf16[8,64,256]{2,1,0:T(8,128)(2,1)} %bitcast.38), calls=%async_computation.8 | async-start | bytes 524288 | tf_op jit(solution)/shard_map/all_to_all | solution.py:34
  133.0 21.4 %all-to-all-start.4 = ((bf16[8,128,256]{2,1,0:T(8,128)(2,1)}), bf16[8,128,256]{2,1,0:T(8,128)(2,1)S(1)}, u32[]{:S(2)}, u32[]{:S(2)}) async-start(bf16[8,128,256]{2,1,0:T(8,128)(2,1)} %bitcast.34), calls=%async_computation.4 | async-start | bytes 1048576 | tf_op jit(solution)/shard_map/all_to_all | solution.py:34
  154.5 22.8 %all-to-all-start.9 = ((bf16[64,16,256]{2,1,0:T(8,128)(2,1)}), bf16[64,16,256]{2,1,0:T(8,128)(2,1)S(1)}, u32[]{:S(2)}, u32[]{:S(2)}) async-start(bf16[64,16,256]{2,1,0:T(8,128)(2,1)} %bitcast.35), calls=%async_computation.9 | async-start | bytes 1048576 | tf_op jit(solution)/shard_map/all_to_all | solution.py:34
  178.1 22.0 %all-to-all-start.5 = ((bf16[8,128,256]{2,1,0:T(8,128)(2,1)}), bf16[8,128,256]{2,1,0:T(8,128)(2,1)S(1)}, u32[]{:S(2)}, u32[]{:S(2)}) async-start(bf16[8,128,256]{2,1,0:T(8,128)(2,1)} %broadcast_in_dim.38), calls=%async_computation.5 | async-start | bytes 1048576 | tf_op jit(solution)/shard_map/all_to_all | solution.py:34

commit v2 on v1

v2 whole, which is shorter than its diff:
```python
import functools

import jax
import jax.numpy as jnp
from jax import lax
from jax.experimental import pallas as pl
from jax.experimental.pallas import tpu as pltpu
from jax.sharding import PartitionSpec as P

BLOCK_CAP = 2


def earlier_equal(keys):
    size = keys.shape[-1]
    before = jnp.arange(size)[None, :] < jnp.arange(size)[:, None]
    same = keys[..., :, None] == keys[..., None, :]
    return jnp.sum((same & before).astype(jnp.int32), axis=-1)


def slot_mask(slots, target):
    return jnp.arange(slots, dtype=jnp.int32)[:, None] == target[None, :]


def pack_ints(mask, values):
    return jnp.max(jnp.where(mask, values[None, :], -1), axis=1)


def select_rows(mask, values, contract=1):
    return lax.dot_general(
        mask.astype(jnp.bfloat16),
        values,
        (((contract,), (0,)), ((), ())),
        preferred_element_type=jnp.float32,
    )


MESH = pl.DeviceIdType.MESH
AXES = ("wide", "narrow")


def meet_peers():
    barrier = pltpu.get_barrier_semaphore()
    count = 0
    for axis in AXES:
        size, me = lax.axis_size(axis), lax.axis_index(axis)

        def greet(step, carry, axis=axis, size=size, me=me):
            peer = lax.rem(me + step, size)
            pl.semaphore_signal(barrier, inc=1, device_id={axis: peer}, device_id_type=MESH)
            return carry

        lax.fori_loop(1, size, greet, 0)
        count += size - 1
    pl.semaphore_wait(barrier, count)


def send_all(axis, pick, dst, send_sem, recv_sem):
    size, me = lax.axis_size(axis), lax.axis_index(axis)

    def send(step, carry):
        peer = lax.rem(me + step, size)
        pltpu.make_async_remote_copy(
            src_ref=pick(peer),
            dst_ref=dst.at[me],
            send_sem=send_sem,
            recv_sem=recv_sem,
            device_id={axis: peer},
            device_id_type=MESH,
        ).start()
        return carry

    lax.fori_loop(1, size, send, 0)


def wait_all(axis, dst, send_sem, recv_sem):
    size, me = lax.axis_size(axis), lax.axis_index(axis)
    rest = dst.at[pl.ds(0, size - 1)]
    pltpu.make_async_remote_copy(
        src_ref=rest,
        dst_ref=rest,
        send_sem=send_sem,
        recv_sem=recv_sem,
        device_id={axis: lax.rem(me + 1, size)},
        device_id_type=MESH,
    ).wait()


def exchange_kernel(axes, *refs):
    count = len(axes)
    srcs, dsts = refs[:count], refs[count : 2 * count]
    send_sems, recv_sems, own_sems = refs[2 * count :]
    meet_peers()
    own = []
    for i, axis in enumerate(axes):
        src = srcs[i]
        send_all(axis, lambda peer, src=src: src.at[peer], dsts[i], send_sems.at[i], recv_sems.at[i])
    for i, axis in enumerate(axes):
        me = lax.axis_index(axis)
        copy = pltpu.make_async_copy(srcs[i].at[me], dsts[i].at[me], own_sems.at[i])
        copy.start()
        own.append(copy)
    for copy in own:
        copy.wait()
    for i, axis in enumerate(axes):
        wait_all(axis, dsts[i], send_sems.at[i], recv_sems.at[i])


def exchange(ident, *pairs):
    axes = tuple(axis for _, axis in pairs)
    values = [value for value, _ in pairs]
    return pl.pallas_call(
        functools.partial(exchange_kernel, axes),
        out_shape=[jax.ShapeDtypeStruct(value.shape, value.dtype) for value in values],
        in_specs=[pl.BlockSpec(memory_space=pl.ANY)] * len(values),
        out_specs=[pl.BlockSpec(memory_space=pl.ANY)] * len(values),
        scratch_shapes=[pltpu.SemaphoreType.DMA((len(values),))] * 3,
        compiler_params=pltpu.CompilerParams(collective_id=ident, has_side_effects=True),
    )(*values)


def finish_kernel(
    block_src, part_src, block_dst, copies, landed, share, send_sems, recv_sems, own_sems
):
    meet_peers()
    wide_me, me = lax.axis_index("wide"), lax.axis_index("narrow")
    send_all("narrow", lambda peer: part_src.at[peer], landed, send_sems.at[0], recv_sems.at[0])
    send_all("wide", lambda peer: block_src.at[peer], block_dst, send_sems.at[1], recv_sems.at[1])
    own_part = pltpu.make_async_copy(part_src.at[me], landed.at[me], own_sems.at[0])
    own_part.start()
    own_block = pltpu.make_async_copy(block_src.at[wide_me], block_dst.at[wide_me], own_sems.at[1])
    own_block.start()
    own_part.wait()
    wait_all("narrow", landed, send_sems.at[0], recv_sems.at[0])
    total = landed[0].astype(jnp.float32)
    for peer in range(1, landed.shape[0]):
        total = total + landed[peer].astype(jnp.float32)
    share[...] = total.astype(share.dtype)
    send_all("narrow", lambda peer: share, copies, send_sems.at[2], recv_sems.at[2])
    own_share = pltpu.make_async_copy(share, copies.at[me], own_sems.at[2])
    own_share.start()
    own_share.wait()
    own_block.wait()
    wait_all("wide", block_dst, send_sems.at[1], recv_sems.at[1])
    wait_all("narrow", copies, send_sems.at[2], recv_sems.at[2])


def finish(ident, block_prod, parts):
    any_space = pl.BlockSpec(memory_space=pl.ANY)
    return pl.pallas_call(
        finish_kernel,
        out_shape=[
            jax.ShapeDtypeStruct(block_prod.shape, block_prod.dtype),
            jax.ShapeDtypeStruct(parts.shape, parts.dtype),
        ],
        in_specs=[any_space] * 2,
        out_specs=[any_space] * 2,
        scratch_shapes=[
            pltpu.VMEM(parts.shape, parts.dtype),
            pltpu.VMEM(parts.shape[1:], parts.dtype),
        ]
        + [pltpu.SemaphoreType.DMA((3,))] * 3,
        compiler_params=pltpu.CompilerParams(collective_id=ident, has_side_effects=True),
    )(block_prod, parts)


def widen(ids):
    return jnp.pad(ids, ((0, 0), (0, 128 - ids.shape[1])), constant_values=-1)[:, None, :]


def on_device(
    quot_owner, quot_row, rem_owner, rem_row, out_grad, quot_table, quot_scale, rem_table
):
    wide_size = lax.axis_size("wide")
    narrow_size = lax.axis_size("narrow")
    tokens, width = out_grad.shape
    quot_slots = 2 * tokens // wide_size
    rem_slots = tokens // narrow_size
    block_slots = BLOCK_CAP * narrow_size
    quot_rows = quot_table.shape[0]
    rows_each = rem_table.shape[0] // wide_size
    quot_owner, rem_owner = quot_owner[:, 0], rem_owner[:, 0]

    rem_target = rem_owner * rem_slots + earlier_equal(rem_owner)
    rem_mask = slot_mask(tokens, rem_target)
    quot_target = quot_owner * quot_slots + earlier_equal(quot_owner)
    quot_mask = slot_mask(wide_size * quot_slots, quot_target)
    got_ids, rem_ids = exchange(
        0,
        (widen(pack_ints(quot_mask, quot_row).reshape(wide_size, quot_slots)), "wide"),
        (widen(pack_ints(rem_mask, rem_row).reshape(narrow_size, rem_slots)), "narrow"),
    )
    got_ids = got_ids[:, 0, :quot_slots].reshape(-1)
    rem_ids = rem_ids[:, 0, :rem_slots]

    grads = out_grad.astype(jnp.float32)
    dequant = (quot_table.astype(jnp.float32) * quot_scale[:, None]).astype(jnp.bfloat16)
    quot_pick = slot_mask(quot_rows, got_ids)
    quot_fetched = select_rows(quot_pick, dequant, 0).astype(jnp.bfloat16)
    rem_fetched = rem_table.at[rem_ids].get(mode="promise_in_bounds")
    block = rem_ids // rows_each
    peers = jnp.arange(narrow_size, dtype=jnp.int32)[:, None]
    block_target = block * block_slots + peers * BLOCK_CAP + earlier_equal(block)
    block_mask = slot_mask(wide_size * block_slots, block_target.reshape(-1))
    block_ids = pack_ints(block_mask, (rem_ids % rows_each).reshape(-1))

    quot_back, returned, block_ids = exchange(
        1,
        (quot_fetched.reshape(wide_size, quot_slots, width), "wide"),
        (rem_fetched, "narrow"),
        (widen(block_ids.reshape(wide_size, block_slots)), "wide"),
    )
    block_ids = block_ids[:, 0, :block_slots].reshape(-1)
    rem_tok = select_rows(rem_mask, returned.reshape(-1, width), 0)
    product = (grads * rem_tok).astype(jnp.bfloat16)
    quot_tok = select_rows(quot_mask, quot_back.reshape(-1, width), 0)
    prod_r = (grads * quot_tok).astype(jnp.bfloat16)
    got_prod, rem_prod = exchange(
        2,
        (
            select_rows(quot_mask, product)
            .astype(jnp.bfloat16)
            .reshape(wide_size, quot_slots, width),
            "wide",
        ),
        (
            select_rows(rem_mask, prod_r)
            .astype(jnp.bfloat16)
            .reshape(narrow_size, rem_slots, width),
            "narrow",
        ),
    )
    block_send = select_rows(block_mask, rem_prod.reshape(-1, width)).astype(jnp.bfloat16)
    partial = select_rows(quot_pick, got_prod.reshape(-1, width)).astype(jnp.bfloat16)
    block_prod, copies = finish(
        3,
        block_send.reshape(wide_size, block_slots, width),
        partial.reshape(narrow_size, -1, width),
    )
    grad_quot = copies.reshape(-1, width).astype(jnp.float32)
    grad_rem = select_rows(slot_mask(rows_each, block_ids), block_prod.reshape(-1, width))
    return (grad_quot, grad_rem[None])


def solution(mesh):
    placed = (
        P(("wide", "narrow"), None),
        P(("wide", "narrow")),
        P(("wide", "narrow"), None),
        P(("wide", "narrow")),
        P(("wide", "narrow"), None),
        P("wide", None),
        P("wide"),
        P("narrow", None),
    )
    return jax.shard_map(
        on_device,
        mesh=mesh,
        in_specs=placed,
        out_specs=(P("wide", None), P("narrow", "wide", None)),
        check_vma=False,
    )
```

time: 203 us -> 127 us (0.63)
  the two profiles are of different devices: /device:TPU:6 before, /device:TPU:16 now
where the time goes in v2:
time: 127 us; the launch traced here: 126 us
  Pallas kernels  98.5 us (78%)
  matrix products  12.6 us (10%)
  other arithmetic  8.25 us (6%)
  local copies, waits for them, and re-layouts  6.14 us (5%)
    pallas_call x3, Pallas kernels, exchange(): pl.pallas_call(functools.partial(exchange_kernel, axes), out_shape=[jax.S...  62.2 us
    pallas_call x1, Pallas kernels, finish(): pl.pallas_call(finish_kernel, out_shape=[jax.ShapeDtypeStruct(block_prod....  36.3 us
    dot_general x6, matrix products, select_rows(): lax.dot_general(mask.astype(jnp.bfloat16), values, (((contract,), (0,)),...  12.6 us
    gather x1, local copies, waits for them, and re-layouts, on_device(): rem_fetched = rem_table.at[rem_ids].get(mode='promise_in_bounds')  2.58 us

profile of v2, /device:TPU:16, one launch (start us, length us, event | category | flops | bytes accessed | tf_op | source)
XLA Modules:
  0.0 126.2 jit_solution(1155350391852276903)
XLA Ops:
  0.6 0.0 copy-start
  0.6 0.0 copy-start.6
  0.7 0.0 copy-start.2
  0.7 1.1 convert_reduce_fusion.1
  1.8 1.0 convert_reduce_fusion
  2.8 0.7 multiply_add_fusion
  3.5 0.9 select_reduce_fusion.2
  4.4 0.1 reshape.203
  4.5 0.6 pad.12
  5.1 0.1 add.76
  5.1 0.1 add.77
  5.2 1.0 select_reduce_fusion.1
  6.3 0.1 reshape.202
  6.3 0.6 pad.11
  7.0 19.2 %shard_map.95 = (s32[64,1,128]{2,1,0:T(1,128)}, s32[8,1,128]{2,1,0:T(1,128)}) custom-call(s32[64,1,128]{2,1,0:T(1,128)} %bitcast.39, s32[8,1,128]{2,1,0:T(1,128)} %bitcast.46), custom_call_target="tpu_custom_call" | custom-call | tf_op jit(solution)/shard_map/pallas_call | solution.py:111
  26.2 0.7 and_select_fusion
  26.9 0.1 squeeze.15
  27.0 0.1 reshape.218
  27.1 0.3 convert_reduce_fusion.2
  27.4 0.1 reduce_sum.32
  27.5 0.4 select_reduce_fusion
  27.9 0.1 reshape.205
  27.9 0.6 pad.13
  28.6 0.8 slice_reduce_fusion.1
  29.4 0.1 eq.129
  29.5 0.0 copy-done
  29.5 2.6 %gather_fusion = bf16[512,256]{1,0:T(8,128)(2,1)} fusion(bf16[4096,256]{1,0:T(8,128)(2,1)S(1)} %copy-done, s32[1024]{0:T(1024)S(1)} %pad_clamp_fusion), kind=kCustom, calls=%fused_computation | custom fusion | bytes 526336 | tf_op jit(solution)/shard_map/gather | solution.py:199
  32.1 0.0 copy-done.6
  32.1 0.0 copy-done.2
  32.1 2.2 %fusion.9 = bf16[1024,256]{1,0:T(8,128)(2,1)} fusion(s32[1024]{0:T(1024)S(1)} %eq.129, bf16[1024,256]{1,0:T(8,128)(2,1)S(1)} %copy-done.2, f32[1024]{0:T(1024)S(1)} %copy-done.6), kind=kOutput, calls=%fused_computation.15 | convolution fusion | flops 538968064 | bytes 1056768 | tf_op jit(solution)/shard_map/dot_general | solution.py:29
  34.3 22.8 %shard_map.96 = (bf16[64,16,256]{2,1,0:T(8,128)(2,1)}, bf16[8,64,256]{2,1,0:T(8,128)(2,1)}, s32[64,1,128]{2,1,0:T(1,128)}) custom-call(bf16[64,16,256]{2,1,0:T(8,128)(2,1)} %bitcast.35, bf16[8,64,256]{2,1,0:T(8,128)(2,1)} %bitcast.31, s32[64,1,128]{2,1,0:T(1,128)} %bitcast.38), custom_call_target="tpu_custom_call" | custom-call | tf_op jit(solution)/shard_map/pallas_call | solution.py:111
  57.1 0.0 copy-start.1
  57.1 0.0 copy-start.4
  57.2 0.0 copy-done.3
  57.2 2.8 %convolution_convert_fusion = bf16[512,256]{1,0:T(8,128)(2,1)} fusion(bf16[1024,256]{1,0:T(8,128)(2,1)} %bitcast.48, s32[512]{0:T(512)S(1)} %get-tuple-element.26, bf16[512,256]{1,0:T(8,128)(2,1)S(1)} %copy-done.3, s32[512]{0:T(512)S(1)} %get-tuple-element.25), kind=kOutput, calls=%fused_computation.19 | convolution fusion | flops 403963904 | bytes 1052672 | tf_op jit(solution)/shard_map/dot_general | solution.py:29
  60.0 0.0 copy-done.1
  60.0 0.1 slice_reduce_fusion
  60.1 0.1 eq.133
  60.2 0.0 copy-done.4
  60.2 1.7 %fusion.8 = bf16[1024,256]{1,0:T(8,128)(2,1)} fusion(bf16[512,256]{1,0:T(8,128)(2,1)S(1)} %bitcast.50, s32[512]{0:T(512)S(1)} %get-tuple-element.26, bf16[512,256]{1,0:T(8,128)(2,1)S(1)} %copy-done.3, s32[512]{0:T(512)S(1)} %get-tuple-element.25), kind=kOutput, calls=%fused_computation.14 | convolution fusion | flops 404094976 | bytes 1052672 | tf_op jit(solution)/shard_map/dot_general | solution.py:29
  61.9 20.1 %shard_map.97 = (bf16[64,16,256]{2,1,0:T(8,128)(2,1)}, bf16[8,64,256]{2,1,0:T(8,128)(2,1)}) custom-call(bf16[64,16,256]{2,1,0:T(8,128)(2,1)} %bitcast.32, bf16[8,64,256]{2,1,0:T(8,128)(2,1)} %bitcast.37), custom_call_target="tpu_custom_call" | custom-call | tf_op jit(solution)/shard_map/pallas_call | solution.py:111
  82.0 0.0 copy-start.5
  82.0 2.7 %fusion.10 = bf16[1024,256]{1,0:T(8,128)(2,1)} fusion(bf16[1024,256]{1,0:T(8,128)(2,1)} %bitcast.49, s32[1024]{0:T(1024)S(1)} %eq.129), kind=kOutput, calls=%fused_computation.16 | convolution fusion | flops 538181632 | bytes 1052672 | tf_op jit(solution)/shard_map/dot_general | solution.py:29
  84.7 0.0 copy-done.5
  84.7 1.3 %fusion.7 = bf16[1024,256]{1,0:T(8,128)(2,1)} fusion(bf16[512,256]{1,0:T(8,128)(2,1)S(1)} %bitcast.51, s32[512]{0:T(512)S(1)} %get-tuple-element.23), kind=kOutput, calls=%fused_computation.13 | convolution fusion | flops 269221888 | bytes 788480 | tf_op jit(solution)/shard_map/dot_general | solution.py:29
  86.0 36.3 %shard_map.98 = (bf16[64,16,256]{2,1,0:T(8,128)(2,1)}, bf16[8,128,256]{2,1,0:T(8,128)(2,1)}) custom-call(bf16[64,16,256]{2,1,0:T(8,128)(2,1)} %bitcast.36, bf16[8,128,256]{2,1,0:T(8,128)(2,1)} %bitcast.34), custom_call_target="tpu_custom_call" | custom-call | tf_op jit(solution)/shard_map/pallas_call | solution.py:149
  122.2 1.9 %convolution_bitcast_fusion = f32[1,64,256]{2,1,0:T(8,128)} fusion(bf16[1024,256]{1,0:T(8,128)(2,1)} %bitcast.33, s32[1024]{0:T(1024)S(1)} %eq.133), kind=kOutput, calls=%fused_computation.22 | convolution fusion | flops 33619968 | bytes 593920 | tf_op jit(solution)/shard_map/dot_general | solution.py:29
  124.1 2.1 %bitcast_convert_fusion = f32[1024,256]{1,0:T(8,128)} fusion(bf16[8,128,256]{2,1,0:T(8,128)(2,1)} %get-tuple-element.17), kind=kLoop, calls=%fused_computation.36 | loop fusion | flops 262144 | bytes 1572864 | tf_op jit(solution)/shard_map/convert_element_type | solution.py:239
  (7 shorter events, 0.1 us)
Async XLA Ops:
  0.6 28.9 %copy-start = (bf16[4096,256]{1,0:T(8,128)(2,1)S(1)}, bf16[4096,256]{1,0:T(8,128)(2,1)}, u32[]{:S(2)}) copy-start(bf16[4096,256]{1,0:T(8,128)(2,1)} %param.15) | copy-start | bytes 6291460
  0.6 31.4 %copy-start.6 = (f32[1024]{0:T(1024)S(1)}, f32[1024]{0:T(1024)}, u32[]{:S(2)}) copy-start(f32[1024]{0:T(1024)} %param.14) | copy-start | bytes 12292
  0.7 31.4 %copy-start.2 = (bf16[1024,256]{1,0:T(8,128)(2,1)S(1)}, bf16[1024,256]{1,0:T(8,128)(2,1)}, u32[]{:S(2)}) copy-start(bf16[1024,256]{1,0:T(8,128)(2,1)} %param.13) | copy-start | bytes 1572868
  32.1 25.1 %copy-start.3 = (bf16[512,256]{1,0:T(8,128)(2,1)S(1)}, bf16[512,256]{1,0:T(8,128)(2,1)}, u32[]{:S(2)}) copy-start(bf16[512,256]{1,0:T(8,128)(2,1)} %param.12) | copy-start | bytes 786436
  57.1 2.9 %copy-start.1 = (s32[64,1,128]{2,1,0:T(1,128)S(1)}, s32[64,1,128]{2,1,0:T(1,128)}, u32[]{:S(2)}) copy-start(s32[64,1,128]{2,1,0:T(1,128)} %get-tuple-element.18) | copy-start | bytes 98308
  57.1 3.0 %copy-start.4 = (bf16[8,64,256]{2,1,0:T(8,128)(2,1)S(1)}, bf16[8,64,256]{2,1,0:T(8,128)(2,1)}, u32[]{:S(2)}) copy-start(bf16[8,64,256]{2,1,0:T(8,128)(2,1)} %get-tuple-element.13) | copy-start | bytes 786436
  82.0 2.7 %copy-start.5 = (bf16[8,64,256]{2,1,0:T(8,128)(2,1)S(1)}, bf16[8,64,256]{2,1,0:T(8,128)(2,1)}, u32[]{:S(2)}) copy-start(bf16[8,64,256]{2,1,0:T(8,128)(2,1)} %get-tuple-element.15) | copy-start | bytes 786436

commit v3 on v1

v3 whole, which is shorter than its diff:
```python
import jax
import jax.numpy as jnp
from jax import lax
from jax.experimental import pallas as pl
from jax.experimental.pallas import tpu as pltpu
from jax.sharding import PartitionSpec as P

BLOCK_CAP = 2


def earlier_equal(keys):
    size = keys.shape[-1]
    before = jnp.arange(size)[None, :] < jnp.arange(size)[:, None]
    same = keys[..., :, None] == keys[..., None, :]
    return jnp.sum((same & before).astype(jnp.int32), axis=-1)


def pack_ints(slots, target, values):
    mask = jnp.arange(slots, dtype=jnp.int32)[:, None] == target[None, :]
    return jnp.max(jnp.where(mask, values[None, :] + 1, 0), axis=1)


def spread(ids, place):
    count = ids.shape[1]
    lane = jnp.arange(LANES, dtype=jnp.int32)[None, :]
    tiled = jnp.tile(ids, (1, LANES // count))
    return jnp.where(lane // count == place % (LANES // count), tiled, 0)[:, None, :]


MESH = pl.DeviceIdType.MESH
AXES = ("wide", "narrow")
LANES = 128


def meet_peers():
    barrier = pltpu.get_barrier_semaphore()
    count = 0
    for axis in AXES:
        size, me = lax.axis_size(axis), lax.axis_index(axis)

        def greet(step, carry, axis=axis, size=size, me=me):
            peer = lax.rem(me + step, size)
            pl.semaphore_signal(barrier, inc=1, device_id={axis: peer}, device_id_type=MESH)
            return carry

        lax.fori_loop(1, size, greet, 0)
        count += size - 1
    pl.semaphore_wait(barrier, count)


def send_all(axis, pick, dst, send_sem, recv_sem):
    size, me = lax.axis_size(axis), lax.axis_index(axis)

    def send(step, carry):
        peer = lax.rem(me + step, size)
        pltpu.make_async_remote_copy(
            src_ref=pick(peer),
            dst_ref=dst.at[me],
            send_sem=send_sem,
            recv_sem=recv_sem,
            device_id={axis: peer},
            device_id_type=MESH,
        ).start()
        return carry

    lax.fori_loop(1, size, send, 0)


def arrivals(axis, dst, send_sem, recv_sem):
    size, me = lax.axis_size(axis), lax.axis_index(axis)
    rest = dst.at[pl.ds(0, size - 1)]
    return pltpu.make_async_remote_copy(
        src_ref=rest,
        dst_ref=rest,
        send_sem=send_sem,
        recv_sem=recv_sem,
        device_id={axis: lax.rem(me + 1, size)},
        device_id_type=MESH,
    )


def one_hot(left, right):
    return jnp.where(left == right, 1.0, 0.0).astype(jnp.bfloat16)


def dot(left, right):
    return jnp.dot(left, right, preferred_element_type=jnp.float32)


def iota(shape, dim):
    return lax.broadcasted_iota(jnp.int32, shape, dim)


def join_ids(landed, joined, groups):
    each = landed.shape[0] // groups
    for group in range(groups):
        row = landed[group * each]
        for peer in range(1, each):
            row = row + landed[group * each + peer]
        joined[group : group + 1, :] = row - 1
    values = joined[...]
    flipped = values.T
    row = jnp.concatenate([values[g : g + 1, :] for g in range(groups)], axis=1)
    col = jnp.concatenate([flipped[:, g : g + 1] for g in range(groups)], axis=0)
    return row, col


def fused_kernel(
    wide_ids_src,
    narrow_ids_src,
    targets_ref,
    grads_ref,
    table_ref,
    scale_ref,
    rem_ref,
    copies,
    grad_rem_ref,
    wide_ids,
    narrow_ids,
    block_ids_src,
    block_ids,
    joined,
    dequant,
    quot_src,
    quot_back,
    rows_src,
    rows_back,
    prod_src,
    prod_got,
    rem_src,
    rem_got,
    block_src,
    block_got,
    pick,
    block_mask,
    part_src,
    parts,
    share,
    send_sems,
    recv_sems,
    own_sem,
):
    wide_me, narrow_me = lax.axis_index("wide"), lax.axis_index("narrow")
    wide_size, narrow_size = wide_ids.shape[0], narrow_ids.shape[0]
    tokens, width = grads_ref.shape
    quot_slots, block_slots = quot_src.shape[1], block_src.shape[1]
    quot_total, block_total = wide_size * quot_slots, wide_size * block_slots
    rem_slots = rows_src.shape[1]
    rows_each = grad_rem_ref.shape[0]
    waits = []

    def ship(axis, src, dst):
        index = len(waits)
        me = wide_me if axis == "wide" else narrow_me
        send_all(axis, lambda peer: src.at[peer], dst, send_sems.at[index], recv_sems.at[index])
        dst[me] = src[me]
        wait = arrivals(axis, dst, send_sems.at[index], recv_sems.at[index])
        waits.append(wait)
        return wait

    joined[...] = jnp.zeros_like(joined)
    meet_peers()
    narrow_ids_wait = ship("narrow", narrow_ids_src, narrow_ids)
    wide_ids_wait = ship("wide", wide_ids_src, wide_ids)

    scales = scale_ref[...].T
    for group in range(scale_ref.shape[0]):
        part = pl.ds(group * LANES, LANES)
        dequant[part, :] = (
            table_ref[part, :].astype(jnp.float32) * scales[:, group : group + 1]
        ).astype(jnp.bfloat16)
    targets = targets_ref[...]
    flipped = targets.T
    quot_row, rem_row = targets[0:1, :], targets[1:2, :]
    quot_col, rem_col = flipped[:, 0:1], flipped[:, 1:2]

    narrow_ids_wait.wait_recv()
    id_row, id_col = join_ids(narrow_ids, joined, tokens // LANES)
    rem_rows = rem_ref.shape[0]
    rows_src[...] = (
        dot(one_hot(id_col, iota((tokens, rem_rows), 1)), rem_ref[...])
        .astype(jnp.bfloat16)
        .reshape(rows_src.shape)
    )
    rows_wait = ship("narrow", rows_src, rows_back)

    wide_ids_wait.wait_recv()
    got_row, got_col = join_ids(wide_ids, joined, quot_total // LANES)
    quot_rows = dequant.shape[0]
    quot_src[...] = (
        dot(one_hot(got_col, iota((quot_total, quot_rows), 1)), dequant[...])
        .astype(jnp.bfloat16)
        .reshape(quot_src.shape)
    )
    quot_wait = ship("wide", quot_src, quot_back)

    each = tokens // narrow_size
    row_block, col_block = id_row // rows_each, id_col // rows_each
    row_place, col_place = iota((1, tokens), 1), iota((tokens, 1), 0)
    alike = (col_block == row_block) & (col_place // each == row_place // each)
    row_rank = jnp.sum(
        jnp.where(alike & (col_place < row_place), 1.0, 0.0), axis=0, keepdims=True
    ).astype(jnp.int32)
    col_rank = jnp.sum(
        jnp.where(alike & (row_place < col_place), 1.0, 0.0), axis=1, keepdims=True
    ).astype(jnp.int32)
    row_slot = (row_place // each) * BLOCK_CAP + row_rank
    col_slot = (col_place // each) * BLOCK_CAP + col_rank
    lane = iota((1, LANES), 1)
    here = lane // block_slots == lax.rem(wide_me, LANES // block_slots)
    offsets = (id_col - col_block * rows_each + 1).astype(jnp.float32)
    spread_ids = jnp.where(
        (col_slot == lax.rem(lane, block_slots)) & here, offsets, 0.0
    ).astype(jnp.bfloat16)
    sent_ids = dot(one_hot(iota((wide_size, 1), 0), row_block), spread_ids).astype(jnp.int32)
    for dest in range(wide_size):
        block_ids_src[dest] = sent_ids[dest : dest + 1, :]
    block_ids_wait = ship("wide", block_ids_src, block_ids)
    block_mask[...] = one_hot(iota((block_total, 1), 0), row_block * block_slots + row_slot)
    pick[...] = one_hot(iota((quot_rows, 1), 0), got_row)

    rows_wait.wait_recv()
    grads = grads_ref[...].astype(jnp.float32)
    rem_tok = dot(
        one_hot(rem_col, iota((tokens, tokens), 1)), rows_back[...].reshape(tokens, width)
    )
    prod_src[...] = (
        dot(one_hot(iota((quot_total, 1), 0), quot_row), (grads * rem_tok).astype(jnp.bfloat16))
        .astype(jnp.bfloat16)
        .reshape(prod_src.shape)
    )
    prod_wait = ship("wide", prod_src, prod_got)

    quot_wait.wait_recv()
    quot_tok = dot(
        one_hot(quot_col, iota((tokens, quot_total), 1)),
        quot_back[...].reshape(quot_total, width),
    )
    rem_src[...] = (
        dot(one_hot(iota((tokens, 1), 0), rem_row), (grads * quot_tok).astype(jnp.bfloat16))
        .astype(jnp.bfloat16)
        .reshape(rem_src.shape)
    )
    rem_wait = ship("narrow", rem_src, rem_got)

    rem_wait.wait_recv()
    block_src[...] = (
        dot(block_mask[...], rem_got[...].reshape(tokens, width))
        .astype(jnp.bfloat16)
        .reshape(block_src.shape)
    )
    block_wait = ship("wide", block_src, block_got)

    prod_wait.wait_recv()
    part_src[...] = (
        dot(pick[...], prod_got[...].reshape(quot_total, width))
        .astype(jnp.bfloat16)
        .reshape(part_src.shape)
    )
    part_wait = ship("narrow", part_src, parts)

    part_wait.wait_recv()
    total = parts[0].astype(jnp.float32)
    for peer in range(1, narrow_size):
        total = total + parts[peer].astype(jnp.float32)
    share[...] = total.astype(jnp.bfloat16)
    index = len(waits)
    send_all("narrow", lambda peer: share, copies, send_sems.at[index], recv_sems.at[index])
    own = pltpu.make_async_copy(share, copies.at[narrow_me], own_sem)
    own.start()
    copies_wait = arrivals("narrow", copies, send_sems.at[index], recv_sems.at[index])
    waits.append(copies_wait)

    block_ids_wait.wait_recv()
    last_row, _ = join_ids(block_ids, joined, block_total // LANES)
    last_mask = one_hot(iota((rows_each, 1), 0), last_row)
    block_wait.wait_recv()
    grad_rem_ref[...] = dot(last_mask, block_got[...].reshape(block_total, width))
    own.wait()
    copies_wait.wait_recv()
    for wait in waits:
        wait.wait_send()


def on_device(
    quot_owner, quot_row, rem_owner, rem_row, out_grad, quot_table, quot_scale, rem_table
):
    wide_size = lax.axis_size("wide")
    narrow_size = lax.axis_size("narrow")
    tokens, width = out_grad.shape
    quot_slots = 2 * tokens // wide_size
    rem_slots = tokens // narrow_size
    block_slots = BLOCK_CAP * narrow_size
    quot_rows = quot_table.shape[0]
    rows_each = rem_table.shape[0] // wide_size
    quot_owner, rem_owner = quot_owner[:, 0], rem_owner[:, 0]

    rem_target = rem_owner * rem_slots + earlier_equal(rem_owner)
    quot_target = quot_owner * quot_slots + earlier_equal(quot_owner)
    wide_ids = spread(
        pack_ints(wide_size * quot_slots, quot_target, quot_row).reshape(wide_size, quot_slots),
        lax.axis_index("wide"),
    )
    narrow_ids = spread(
        pack_ints(tokens, rem_target, rem_row).reshape(narrow_size, rem_slots),
        lax.axis_index("narrow"),
    )
    targets = jnp.zeros((8, tokens), jnp.int32).at[0].set(quot_target).at[1].set(rem_target)

    half = jnp.bfloat16
    wide_shape = pltpu.VMEM((wide_size, quot_slots, width), half)
    narrow_shape = pltpu.VMEM((narrow_size, rem_slots, width), half)
    block_shape = pltpu.VMEM((wide_size, block_slots, width), half)
    part = (narrow_size, quot_rows // narrow_size, width)
    whole = pl.BlockSpec(memory_space=pltpu.VMEM)
    copies, grad_rem = pl.pallas_call(
        fused_kernel,
        out_shape=[
            jax.ShapeDtypeStruct(part, half),
            jax.ShapeDtypeStruct((rows_each, width), jnp.float32),
        ],
        in_specs=[whole] * 7,
        out_specs=[pl.BlockSpec(memory_space=pl.ANY), whole],
        scratch_shapes=[
            pltpu.VMEM(wide_ids.shape, jnp.int32),
            pltpu.VMEM(narrow_ids.shape, jnp.int32),
            pltpu.VMEM(wide_ids.shape, jnp.int32),
            pltpu.VMEM(wide_ids.shape, jnp.int32),
            pltpu.VMEM((8, LANES), jnp.int32),
            pltpu.VMEM((quot_rows, width), half),
            wide_shape,
            wide_shape,
            narrow_shape,
            narrow_shape,
            wide_shape,
            wide_shape,
            narrow_shape,
            narrow_shape,
            block_shape,
            block_shape,
            pltpu.VMEM((quot_rows, wide_size * quot_slots), half),
            pltpu.VMEM((wide_size * block_slots, tokens), half),
            pltpu.VMEM(part, half),
            pltpu.VMEM(part, half),
            pltpu.VMEM(part[1:], half),
            pltpu.SemaphoreType.DMA((10,)),
            pltpu.SemaphoreType.DMA((10,)),
            pltpu.SemaphoreType.DMA,
        ],
        compiler_params=pltpu.CompilerParams(collective_id=0, has_side_effects=True),
    )(
        wide_ids,
        narrow_ids,
        targets,
        out_grad,
        quot_table,
        quot_scale.reshape(-1, LANES),
        rem_table,
    )
    return (copies.reshape(-1, width).astype(jnp.float32), grad_rem[None])


def solution(mesh):
    placed = (
        P(("wide", "narrow"), None),
        P(("wide", "narrow")),
        P(("wide", "narrow"), None),
        P(("wide", "narrow")),
        P(("wide", "narrow"), None),
        P("wide", None),
        P("wide"),
        P("narrow", None),
    )
    return jax.shard_map(
        on_device,
        mesh=mesh,
        in_specs=placed,
        out_specs=(P("wide", None), P("narrow", "wide", None)),
        check_vma=False,
    )
```

time: 203 us -> 95.1 us (0.47)
  waiting for transfers between devices: 112 us -> 0 us
  Pallas kernels: 0 us -> 83.3 us
  starting transfers between devices: 61 us -> 0 us
  matrix products: 11.3 us -> 0 us
  local copies, waits for them, and re-layouts: 6.59 us -> 1.94 us
    all_to_all x10 -> x0, waiting for transfers between devices: 112 us -> none  [exchange(): return lax.all_to_all(value, axis, split_axis=0, concat_axis=0, tiled=True)]
    pallas_call x0 -> x1, Pallas kernels: none -> 83.3 us  [on_device(): pl.pallas_call(fused_kernel, out_shape=[jax.ShapeDtypeStruct(part, half),...]
    all_to_all x10 -> x0, starting transfers between devices: 61 us -> none  [exchange(): return lax.all_to_all(value, axis, split_axis=0, concat_axis=0, tiled=True)]
    dot_general x6 -> x0, matrix products: 11.3 us -> none  [select_rows(): lax.dot_general(mask.astype(jnp.bfloat16), values, (((contract,), (0,)),...]
    all_to_all x5 -> x0, local copies, waits for them, and re-layouts: 2.71 us -> none  [exchange(): return lax.all_to_all(value, axis, split_axis=0, concat_axis=0, tiled=True)]
    gather x1 -> x0, local copies, waits for them, and re-layouts: 2.58 us -> none  [on_device(): fetched = rem_table.at[rem_ids].get(mode='promise_in_bounds')]
    all_to_all x3 -> x0, other arithmetic: 2.26 us -> none  [exchange(): return lax.all_to_all(value, axis, split_axis=0, concat_axis=0, tiled=True)]
  transfers between devices with their start and end apart: 10 -> 0, of which waited for: 10 -> 0; matrix products, arithmetic and copies ran while one was open for 10% -> 0% of each run, Pallas kernels for 0% -> 0%
where the time goes in v3:
time: 95.1 us; the launch traced here: 94.7 us
  Pallas kernels  83.3 us (88%)
  other arithmetic  8.73 us (9%)
  local copies, waits for them, and re-layouts  1.94 us (2%)
    pallas_call x1, Pallas kernels, on_device(): pl.pallas_call(fused_kernel, out_shape=[jax.ShapeDtypeStruct(part, half),...  83.3 us
    convert_element_type x1, other arithmetic, on_device(): return (copies.reshape(-1, width).astype(jnp.float32), grad_rem[None])  2.09 us
    reduce_sum x2, other arithmetic, earlier_equal(): return jnp.sum((same & before).astype(jnp.int32), axis=-1)  2.01 us

profile of v3, /device:TPU:6, one launch (start us, length us, event | category | flops | bytes accessed | tf_op | source)
XLA Modules:
  0.0 94.7 jit_solution(6451962124227368470)
XLA Ops:
  0.7 1.0 %convert_reduce_fusion.1 = s32[512]{0:T(512)S(1)} fusion(s32[512]{0:T(512)} %bitcast.18), kind=kLoop, calls=%fused_computation.5 | loop fusion | flops 1310208 | bytes 4096 | tf_op jit(solution)/shard_map/reduce_sum | solution.py:15
  1.7 1.0 %convert_reduce_fusion = s32[512]{0:T(512)S(1)} fusion(s32[512]{0:T(512)} %bitcast.16), kind=kLoop, calls=%fused_computation.3 | loop fusion | flops 1310208 | bytes 4096 | tf_op jit(solution)/shard_map/reduce_sum | solution.py:15
  2.7 0.7 bitcast_add_fusion
  3.4 0.7 bitcast_add_fusion.1
  4.1 0.7 multiply_add_fusion
  4.8 0.2 select_reduce_fusion.1
  5.0 0.1 tile.23
  5.1 0.1 tile.25
  5.2 0.6 broadcast_select_fusion.1.narrow_ids_src
  5.8 0.7 multiply_add_fusion.1
  6.5 0.4 select_reduce_fusion
  6.8 0.1 scatter.9.targets_ref
  6.9 0.0 copy-start
  6.9 0.1 tile.20
  7.0 0.1 copy.12
  7.1 0.1 copy.13
  7.1 0.7 broadcast_select_fusion.wide_ids_src
  7.8 0.0 copy-done
  7.8 83.3 %shard_map.95 = (bf16[8,128,256]{2,1,0:T(8,128)(2,1)}, f32[64,256]{1,0:T(8,128)}) custom-call(s32[64,1,128]{2,1,0:T(1,128)} %broadcast_select_fusion.wide_ids_src, s32[8,1,128]{2,1,0:T(1,128)} %broadcast_select_fusion.1.narrow_ids_src, s32[8,512]{1,0:T(8,128)} %copy-done, bf16[512,256]{1,0:T(8,128)(2,1)} %grads_ref.1, bf16[1024,256]{1,0:T(8,128)(2,1)} %table_ref.1, ...), custom_call_target="tpu_custom_call" | custom-call | tf_op jit(solution)/shard_map/pallas_call | solution.py:316
  91.1 2.1 %bitcast_convert_fusion = f32[1024,256]{1,0:T(8,128)} fusion(bf16[8,128,256]{2,1,0:T(8,128)(2,1)} %get-tuple-element.28), kind=kLoop, calls=%fused_computation.9 | loop fusion | flops 262144 | bytes 1572864 | tf_op jit(solution)/shard_map/convert_element_type | solution.py:360
  93.2 1.5 %copy.16 = f32[1,64,256]{2,1,0:T(8,128)} copy(f32[1,64,256]{2,1,0:T(8,128)} %bitcast.15) | data formatting | bytes 131072
  (5 shorter events, 0.0 us)
Async XLA Ops:
  6.9 0.9 copy-start

commit v4 on v3

--- a/solution.py
+++ b/solution.py
@@ -8,31 +8,13 @@
 BLOCK_CAP = 2
 
 
-def earlier_equal(keys):
-    size = keys.shape[-1]
-    before = jnp.arange(size)[None, :] < jnp.arange(size)[:, None]
-    same = keys[..., :, None] == keys[..., None, :]
-    return jnp.sum((same & before).astype(jnp.int32), axis=-1)
-
-
-def pack_ints(slots, target, values):
-    mask = jnp.arange(slots, dtype=jnp.int32)[:, None] == target[None, :]
-    return jnp.max(jnp.where(mask, values[None, :] + 1, 0), axis=1)
-
-
-def spread(ids, place):
-    count = ids.shape[1]
-    lane = jnp.arange(LANES, dtype=jnp.int32)[None, :]
-    tiled = jnp.tile(ids, (1, LANES // count))
-    return jnp.where(lane // count == place % (LANES // count), tiled, 0)[:, None, :]
-
-
 MESH = pl.DeviceIdType.MESH
 AXES = ("wide", "narrow")
 LANES = 128
-
-
-def meet_peers():
+PIECES = 4
+
+
+def greet_peers():
     barrier = pltpu.get_barrier_semaphore()
     count = 0
     for axis in AXES:
@@ -45,17 +27,17 @@
 
         lax.fori_loop(1, size, greet, 0)
         count += size - 1
-    pl.semaphore_wait(barrier, count)
-
-
-def send_all(axis, pick, dst, send_sem, recv_sem):
+    return barrier, count
+
+
+def send_all(axis, pick, dst, send_sem, recv_sem, land=lambda dst, me: dst.at[me]):
     size, me = lax.axis_size(axis), lax.axis_index(axis)
 
     def send(step, carry):
         peer = lax.rem(me + step, size)
         pltpu.make_async_remote_copy(
             src_ref=pick(peer),
-            dst_ref=dst.at[me],
+            dst_ref=land(dst, me),
             send_sem=send_sem,
             recv_sem=recv_sem,
             device_id={axis: peer},
@@ -66,9 +48,9 @@
     lax.fori_loop(1, size, send, 0)
 
 
-def arrivals(axis, dst, send_sem, recv_sem):
+def arrivals(axis, dst, send_sem, recv_sem, land=lambda dst, rows: dst.at[rows]):
     size, me = lax.axis_size(axis), lax.axis_index(axis)
-    rest = dst.at[pl.ds(0, size - 1)]
+    rest = land(dst, pl.ds(0, size - 1))
     return pltpu.make_async_remote_copy(
         src_ref=rest,
         dst_ref=rest,
@@ -89,6 +71,33 @@
 
 def iota(shape, dim):
     return lax.broadcasted_iota(jnp.int32, shape, dim)
+
+
+def ranks(alike):
+    size = alike.shape[0]
+    rows, cols = iota((1, size), 1), iota((size, 1), 0)
+    row_rank = jnp.sum(jnp.where(alike & (cols < rows), 1.0, 0.0), axis=0, keepdims=True)
+    col_rank = jnp.sum(jnp.where(alike & (rows < cols), 1.0, 0.0), axis=1, keepdims=True)
+    return row_rank.astype(jnp.int32), col_rank.astype(jnp.int32)
+
+
+def spread_ids(dests, dest_row, count, place, slot_col, value_col):
+    lane = iota((1, LANES), 1)
+    here = lane // count == lax.rem(place, LANES // count)
+    spot = (slot_col == lax.rem(lane, count)) & here
+    mask = one_hot(iota((dests, 1), 0), dest_row)
+    value = value_col + 1
+    high = value // 64
+
+    def gather(digit):
+        return dot(mask, jnp.where(spot, digit.astype(jnp.float32), 0.0).astype(jnp.bfloat16))
+
+    return (gather(high) * 64.0 + gather(value - high * 64)).astype(jnp.int32)
+
+
+def store_rows(dst, values):
+    for row in range(dst.shape[0]):
+        dst[row] = values[row : row + 1, :]
 
 
 def join_ids(landed, joined, groups):
@@ -106,15 +115,19 @@
 
 
 def fused_kernel(
-    wide_ids_src,
-    narrow_ids_src,
-    targets_ref,
+    quot_owner_ref,
+    quot_row_ref,
+    rem_owner_ref,
+    rem_row_ref,
     grads_ref,
     table_ref,
     scale_ref,
     rem_ref,
     copies,
     grad_rem_ref,
+    facts,
+    wide_ids_src,
+    narrow_ids_src,
     wide_ids,
     narrow_ids,
     block_ids_src,
@@ -138,7 +151,7 @@
     share,
     send_sems,
     recv_sems,
-    own_sem,
+    own_sems,
 ):
     wide_me, narrow_me = lax.axis_index("wide"), lax.axis_index("narrow")
     wide_size, narrow_size = wide_ids.shape[0], narrow_ids.shape[0]
@@ -158,8 +171,30 @@
         waits.append(wait)
         return wait
 
+    barrier, greeted = greet_peers()
     joined[...] = jnp.zeros_like(joined)
-    meet_peers()
+    facts[...] = jnp.zeros_like(facts)
+    inputs = (quot_owner_ref, quot_row_ref, rem_owner_ref, rem_row_ref)
+    for row, ref in enumerate(inputs):
+        facts[row : row + 1, :] = ref[...]
+    flipped = facts[...].T
+    quot_owner, rem_owner = quot_owner_ref[...], rem_owner_ref[...]
+    quot_owner_col, quot_value = flipped[:, 0:1], flipped[:, 1:2]
+    rem_owner_col, rem_value = flipped[:, 2:3], flipped[:, 3:4]
+    row_rank, col_rank = ranks(rem_owner_col == rem_owner)
+    rem_row, rem_col = rem_owner * rem_slots + row_rank, rem_owner_col * rem_slots + col_rank
+    store_rows(
+        narrow_ids_src,
+        spread_ids(narrow_size, rem_owner, rem_slots, narrow_me, col_rank, rem_value),
+    )
+    row_rank, col_rank = ranks(quot_owner_col == quot_owner)
+    quot_row = quot_owner * quot_slots + row_rank
+    quot_col = quot_owner_col * quot_slots + col_rank
+    store_rows(
+        wide_ids_src,
+        spread_ids(wide_size, quot_owner, quot_slots, wide_me, col_rank, quot_value),
+    )
+    pl.semaphore_wait(barrier, greeted)
     narrow_ids_wait = ship("narrow", narrow_ids_src, narrow_ids)
     wide_ids_wait = ship("wide", wide_ids_src, wide_ids)
 
@@ -169,11 +204,6 @@
         dequant[part, :] = (
             table_ref[part, :].astype(jnp.float32) * scales[:, group : group + 1]
         ).astype(jnp.bfloat16)
-    targets = targets_ref[...]
-    flipped = targets.T
-    quot_row, rem_row = targets[0:1, :], targets[1:2, :]
-    quot_col, rem_col = flipped[:, 0:1], flipped[:, 1:2]
-
     narrow_ids_wait.wait_recv()
     id_row, id_col = join_ids(narrow_ids, joined, tokens // LANES)
     rem_rows = rem_ref.shape[0]
@@ -198,23 +228,14 @@
     row_block, col_block = id_row // rows_each, id_col // rows_each
     row_place, col_place = iota((1, tokens), 1), iota((tokens, 1), 0)
     alike = (col_block == row_block) & (col_place // each == row_place // each)
-    row_rank = jnp.sum(
-        jnp.where(alike & (col_place < row_place), 1.0, 0.0), axis=0, keepdims=True
-    ).astype(jnp.int32)
-    col_rank = jnp.sum(
-        jnp.where(alike & (row_place < col_place), 1.0, 0.0), axis=1, keepdims=True
-    ).astype(jnp.int32)
+    row_rank, col_rank = ranks(alike)
     row_slot = (row_place // each) * BLOCK_CAP + row_rank
     col_slot = (col_place // each) * BLOCK_CAP + col_rank
-    lane = iota((1, LANES), 1)
-    here = lane // block_slots == lax.rem(wide_me, LANES // block_slots)
-    offsets = (id_col - col_block * rows_each + 1).astype(jnp.float32)
-    spread_ids = jnp.where(
-        (col_slot == lax.rem(lane, block_slots)) & here, offsets, 0.0
-    ).astype(jnp.bfloat16)
-    sent_ids = dot(one_hot(iota((wide_size, 1), 0), row_block), spread_ids).astype(jnp.int32)
-    for dest in range(wide_size):
-        block_ids_src[dest] = sent_ids[dest : dest + 1, :]
+    offsets = id_col - col_block * rows_each
+    store_rows(
+        block_ids_src,
+        spread_ids(wide_size, row_block, block_slots, wide_me, col_slot, offsets),
+    )
     block_ids_wait = ship("wide", block_ids_src, block_ids)
     block_mask[...] = one_hot(iota((block_total, 1), 0), row_block * block_slots + row_slot)
     pick[...] = one_hot(iota((quot_rows, 1), 0), got_row)
@@ -257,27 +278,49 @@
         .astype(jnp.bfloat16)
         .reshape(part_src.shape)
     )
-    part_wait = ship("narrow", part_src, parts)
-
-    part_wait.wait_recv()
-    total = parts[0].astype(jnp.float32)
-    for peer in range(1, narrow_size):
-        total = total + parts[peer].astype(jnp.float32)
-    share[...] = total.astype(jnp.bfloat16)
-    index = len(waits)
-    send_all("narrow", lambda peer: share, copies, send_sems.at[index], recv_sems.at[index])
-    own = pltpu.make_async_copy(share, copies.at[narrow_me], own_sem)
-    own.start()
-    copies_wait = arrivals("narrow", copies, send_sems.at[index], recv_sems.at[index])
-    waits.append(copies_wait)
+    step = part_src.shape[1] // PIECES
+    part_waits, copy_waits, owns = [], [], []
+    for piece in range(PIECES):
+        rows, index = pl.ds(piece * step, step), len(waits)
+
+        def land(dst, where, rows=rows):
+            return dst.at[where, rows]
+
+        sems = send_sems.at[index], recv_sems.at[index]
+        send_all("narrow", lambda peer: land(part_src, peer), parts, *sems, land)
+        wait = arrivals("narrow", parts, *sems, land)
+        part_waits.append(wait)
+        waits.append(wait)
+    parts[narrow_me] = part_src[narrow_me]
+    for piece in range(PIECES):
+        rows, index = pl.ds(piece * step, step), len(waits)
+
+        def land(dst, where, rows=rows):
+            return dst.at[where, rows]
+
+        part_waits[piece].wait_recv()
+        total = parts[0, rows, :].astype(jnp.float32)
+        for peer in range(1, narrow_size):
+            total = total + parts[peer, rows, :].astype(jnp.float32)
+        share[rows, :] = total.astype(jnp.bfloat16)
+        sems = send_sems.at[index], recv_sems.at[index]
+        send_all("narrow", lambda peer: share.at[rows], copies, *sems, land)
+        own = pltpu.make_async_copy(share.at[rows], land(copies, narrow_me), own_sems.at[piece])
+        own.start()
+        owns.append(own)
+        wait = arrivals("narrow", copies, *sems, land)
+        copy_waits.append(wait)
+        waits.append(wait)
 
     block_ids_wait.wait_recv()
     last_row, _ = join_ids(block_ids, joined, block_total // LANES)
     last_mask = one_hot(iota((rows_each, 1), 0), last_row)
     block_wait.wait_recv()
     grad_rem_ref[...] = dot(last_mask, block_got[...].reshape(block_total, width))
-    own.wait()
-    copies_wait.wait_recv()
+    for own in owns:
+        own.wait()
+    for wait in copy_waits:
+        wait.wait_recv()
     for wait in waits:
         wait.wait_send()
 
@@ -293,21 +336,9 @@
     block_slots = BLOCK_CAP * narrow_size
     quot_rows = quot_table.shape[0]
     rows_each = rem_table.shape[0] // wide_size
-    quot_owner, rem_owner = quot_owner[:, 0], rem_owner[:, 0]
-
-    rem_target = rem_owner * rem_slots + earlier_equal(rem_owner)
-    quot_target = quot_owner * quot_slots + earlier_equal(quot_owner)
-    wide_ids = spread(
-        pack_ints(wide_size * quot_slots, quot_target, quot_row).reshape(wide_size, quot_slots),
-        lax.axis_index("wide"),
-    )
-    narrow_ids = spread(
-        pack_ints(tokens, rem_target, rem_row).reshape(narrow_size, rem_slots),
-        lax.axis_index("narrow"),
-    )
-    targets = jnp.zeros((8, tokens), jnp.int32).at[0].set(quot_target).at[1].set(rem_target)
-
     half = jnp.bfloat16
+    wide_ids = pltpu.VMEM((wide_size, 1, LANES), jnp.int32)
+    narrow_ids = pltpu.VMEM((narrow_size, 1, LANES), jnp.int32)
     wide_shape = pltpu.VMEM((wide_size, quot_slots, width), half)
     narrow_shape = pltpu.VMEM((narrow_size, rem_slots, width), half)
     block_shape = pltpu.VMEM((wide_size, block_slots, width), half)
@@ -319,13 +350,16 @@
             jax.ShapeDtypeStruct(part, half),
             jax.ShapeDtypeStruct((rows_each, width), jnp.float32),
         ],
-        in_specs=[whole] * 7,
+        in_specs=[whole] * 8,
         out_specs=[pl.BlockSpec(memory_space=pl.ANY), whole],
         scratch_shapes=[
-            pltpu.VMEM(wide_ids.shape, jnp.int32),
-            pltpu.VMEM(narrow_ids.shape, jnp.int32),
-            pltpu.VMEM(wide_ids.shape, jnp.int32),
-            pltpu.VMEM(wide_ids.shape, jnp.int32),
+            pltpu.VMEM((8, tokens), jnp.int32),
+            wide_ids,
+            narrow_ids,
+            wide_ids,
+            narrow_ids,
+            wide_ids,
+            wide_ids,
             pltpu.VMEM((8, LANES), jnp.int32),
             pltpu.VMEM((quot_rows, width), half),
             wide_shape,
@@ -343,15 +377,16 @@
             pltpu.VMEM(part, half),
             pltpu.VMEM(part, half),
             pltpu.VMEM(part[1:], half),
-            pltpu.SemaphoreType.DMA((10,)),
-            pltpu.SemaphoreType.DMA((10,)),
-            pltpu.SemaphoreType.DMA,
+            pltpu.SemaphoreType.DMA((8 + 2 * PIECES,)),
+            pltpu.SemaphoreType.DMA((8 + 2 * PIECES,)),
+            pltpu.SemaphoreType.DMA((PIECES,)),
         ],
         compiler_params=pltpu.CompilerParams(collective_id=0, has_side_effects=True),
     )(
-        wide_ids,
-        narrow_ids,
-        targets,
+        quot_owner.reshape(1, -1),
+        quot_row.reshape(1, -1),
+        rem_owner.reshape(1, -1),
+        rem_row.reshape(1, -1),
         out_grad,
         quot_table,
         quot_scale.reshape(-1, LANES),

time: 95.1 us -> 84.9 us (0.89)
  other arithmetic: 8.73 us -> 2.09 us
  Pallas kernels: 83.3 us -> 80.5 us
    pallas_call x1, Pallas kernels: 83.3 us -> 80.5 us  [on_device(): pl.pallas_call(fused_kernel, out_shape=[jax.ShapeDtypeStruct(part, half),...]
    add x4 -> x0, other arithmetic: 2.78 us -> none  [the longest x2 1.39 us: on_device(): rem_target = rem_owner * rem_slots + earlier_equal(rem_owner)]
    reduce_sum x2 -> x0, other arithmetic: 2.01 us -> none  [earlier_equal(): return jnp.sum((same & before).astype(jnp.int32), axis=-1)]
    select_n x2 -> x0, other arithmetic: 1.27 us -> none  [spread(): jnp.where(lane // count == place % (LANES // count), tiled, 0)[:, None, :]]
where the time goes in v4:
time: 84.9 us; the launch traced here: 84.7 us
  Pallas kernels  80.5 us (95%)
  other arithmetic  2.09 us (2%)
  local copies, waits for them, and re-layouts  1.47 us (2%)
    pallas_call x1, Pallas kernels, on_device(): pl.pallas_call(fused_kernel, out_shape=[jax.ShapeDtypeStruct(part, half),...  80.5 us
    convert_element_type x1, other arithmetic, on_device(): return (copies.reshape(-1, width).astype(jnp.float32), grad_rem[None])  2.09 us

profile of v4, /device:TPU:6, one launch (start us, length us, event | category | flops | bytes accessed | tf_op | source)
XLA Modules:
  0.0 84.7 jit_solution(6505970875686237384)
XLA Ops:
  0.6 80.5 %shard_map.95 = (bf16[8,128,256]{2,1,0:T(8,128)(2,1)}, f32[64,256]{1,0:T(8,128)}) custom-call(s32[1,512]{1,0:T(1,128)} %bitcast.11, s32[1,512]{1,0:T(1,128)} %bitcast.12, s32[1,512]{1,0:T(1,128)} %bitcast.13, s32[1,512]{1,0:T(1,128)} %bitcast.14, bf16[512,256]{1,0:T(8,128)(2,1)} %grads_ref.1, bf16[1024,256]{1,0:T(8,128)(2,1)} %table_ref.1, ...), custom_call_target="tpu_custom_call" | custom-call | tf_op jit(solution)/shard_map/pallas_call | solution.py:347
  81.1 2.1 %bitcast_convert_fusion = f32[1024,256]{1,0:T(8,128)} fusion(bf16[8,128,256]{2,1,0:T(8,128)(2,1)} %get-tuple-element.4), kind=kLoop, calls=%fused_computation | loop fusion | flops 262144 | bytes 1572864 | tf_op jit(solution)/shard_map/convert_element_type | solution.py:395
  83.2 1.5 %copy.11 = f32[1,64,256]{2,1,0:T(8,128)} copy(f32[1,64,256]{2,1,0:T(8,128)} %bitcast.9) | data formatting | bytes 131072

commit v5 on v4

--- a/solution.py
+++ b/solution.py
@@ -11,7 +11,7 @@
 MESH = pl.DeviceIdType.MESH
 AXES = ("wide", "narrow")
 LANES = 128
-PIECES = 4
+PIECES = 2
 
 
 def greet_peers():
@@ -119,12 +119,16 @@
     quot_row_ref,
     rem_owner_ref,
     rem_row_ref,
+    grads_src,
+    table_src,
+    scale_ref,
+    table_rem,
+    copies_left,
+    copies_right,
+    grad_rem_ref,
     grads_ref,
     table_ref,
-    scale_ref,
     rem_ref,
-    copies,
-    grad_rem_ref,
     facts,
     wide_ids_src,
     narrow_ids_src,
@@ -138,20 +142,26 @@
     quot_back,
     rows_src,
     rows_back,
-    prod_src,
-    prod_got,
+    prod_left,
+    prod_right,
+    got_left,
+    got_right,
     rem_src,
     rem_got,
     block_src,
     block_got,
     pick,
     block_mask,
-    part_src,
-    parts,
-    share,
+    part_left,
+    part_right,
+    parts_left,
+    parts_right,
+    share_left,
+    share_right,
     send_sems,
     recv_sems,
     own_sems,
+    load_sems,
 ):
     wide_me, narrow_me = lax.axis_index("wide"), lax.axis_index("narrow")
     wide_size, narrow_size = wide_ids.shape[0], narrow_ids.shape[0]
@@ -171,6 +181,13 @@
         waits.append(wait)
         return wait
 
+    loads = []
+    for index, pair in enumerate(
+        ((table_rem, rem_ref), (table_src, table_ref), (grads_src, grads_ref))
+    ):
+        load = pltpu.make_async_copy(*pair, load_sems.at[index])
+        load.start()
+        loads.append(load)
     barrier, greeted = greet_peers()
     joined[...] = jnp.zeros_like(joined)
     facts[...] = jnp.zeros_like(facts)
@@ -198,6 +215,8 @@
     narrow_ids_wait = ship("narrow", narrow_ids_src, narrow_ids)
     wide_ids_wait = ship("wide", wide_ids_src, wide_ids)
 
+    for load in loads:
+        load.wait()
     scales = scale_ref[...].T
     for group in range(scale_ref.shape[0]):
         part = pl.ds(group * LANES, LANES)
@@ -245,12 +264,14 @@
     rem_tok = dot(
         one_hot(rem_col, iota((tokens, tokens), 1)), rows_back[...].reshape(tokens, width)
     )
-    prod_src[...] = (
-        dot(one_hot(iota((quot_total, 1), 0), quot_row), (grads * rem_tok).astype(jnp.bfloat16))
-        .astype(jnp.bfloat16)
-        .reshape(prod_src.shape)
-    )
-    prod_wait = ship("wide", prod_src, prod_got)
+    half = width // 2
+    packed = dot(
+        one_hot(iota((quot_total, 1), 0), quot_row), (grads * rem_tok).astype(jnp.bfloat16)
+    ).astype(jnp.bfloat16)
+    prod_left[...] = packed[:, :half].reshape(prod_left.shape)
+    left_wait = ship("wide", prod_left, got_left)
+    prod_right[...] = packed[:, half:].reshape(prod_right.shape)
+    right_wait = ship("wide", prod_right, got_right)
 
     quot_wait.wait_recv()
     quot_tok = dot(
@@ -263,6 +284,51 @@
         .reshape(rem_src.shape)
     )
     rem_wait = ship("narrow", rem_src, rem_got)
+
+    step = part_left.shape[1] // PIECES
+
+    def piece_of(piece):
+        rows = pl.ds(piece * step, step)
+        return rows, lambda dst, where: dst.at[where, rows]
+
+    def reduce_parts(got, part_src, parts):
+        part_src[...] = (
+            dot(pick[...], got[...].reshape(quot_total, half))
+            .astype(jnp.bfloat16)
+            .reshape(part_src.shape)
+        )
+        started = []
+        for piece in range(PIECES):
+            rows, land = piece_of(piece)
+            sems = send_sems.at[len(waits)], recv_sems.at[len(waits)]
+            send_all("narrow", lambda peer: land(part_src, peer), parts, *sems, land)
+            started.append(arrivals("narrow", parts, *sems, land))
+            waits.append(started[-1])
+        parts[narrow_me] = part_src[narrow_me]
+        return started
+
+    owns, copy_waits = [], []
+
+    def send_back(started, parts, share, copies):
+        for piece in range(PIECES):
+            rows, land = piece_of(piece)
+            started[piece].wait_recv()
+            total = parts[0, rows, :].astype(jnp.float32)
+            for peer in range(1, narrow_size):
+                total = total + parts[peer, rows, :].astype(jnp.float32)
+            share[rows, :] = total.astype(jnp.bfloat16)
+            sems = send_sems.at[len(waits)], recv_sems.at[len(waits)]
+            send_all("narrow", lambda peer: share.at[rows], copies, *sems, land)
+            own = pltpu.make_async_copy(
+                share.at[rows], land(copies, narrow_me), own_sems.at[len(owns)]
+            )
+            own.start()
+            owns.append(own)
+            copy_waits.append(arrivals("narrow", copies, *sems, land))
+            waits.append(copy_waits[-1])
+
+    left_wait.wait_recv()
+    left_started = reduce_parts(got_left, part_left, parts_left)
 
     rem_wait.wait_recv()
     block_src[...] = (
@@ -272,45 +338,10 @@
     )
     block_wait = ship("wide", block_src, block_got)
 
-    prod_wait.wait_recv()
-    part_src[...] = (
-        dot(pick[...], prod_got[...].reshape(quot_total, width))
-        .astype(jnp.bfloat16)
-        .reshape(part_src.shape)
-    )
-    step = part_src.shape[1] // PIECES
-    part_waits, copy_waits, owns = [], [], []
-    for piece in range(PIECES):
-        rows, index = pl.ds(piece * step, step), len(waits)
-
-        def land(dst, where, rows=rows):
-            return dst.at[where, rows]
-
-        sems = send_sems.at[index], recv_sems.at[index]
-        send_all("narrow", lambda peer: land(part_src, peer), parts, *sems, land)
-        wait = arrivals("narrow", parts, *sems, land)
-        part_waits.append(wait)
-        waits.append(wait)
-    parts[narrow_me] = part_src[narrow_me]
-    for piece in range(PIECES):
-        rows, index = pl.ds(piece * step, step), len(waits)
-
-        def land(dst, where, rows=rows):
-            return dst.at[where, rows]
-
-        part_waits[piece].wait_recv()
-        total = parts[0, rows, :].astype(jnp.float32)
-        for peer in range(1, narrow_size):
-            total = total + parts[peer, rows, :].astype(jnp.float32)
-        share[rows, :] = total.astype(jnp.bfloat16)
-        sems = send_sems.at[index], recv_sems.at[index]
-        send_all("narrow", lambda peer: share.at[rows], copies, *sems, land)
-        own = pltpu.make_async_copy(share.at[rows], land(copies, narrow_me), own_sems.at[piece])
-        own.start()
-        owns.append(own)
-        wait = arrivals("narrow", copies, *sems, land)
-        copy_waits.append(wait)
-        waits.append(wait)
+    right_wait.wait_recv()
+    right_started = reduce_parts(got_right, part_right, parts_right)
+    send_back(left_started, parts_left, share_left, copies_left)
+    send_back(right_started, parts_right, share_right, copies_right)
 
     block_ids_wait.wait_recv()
     last_row, _ = join_ids(block_ids, joined, block_total // LANES)
@@ -323,6 +354,30 @@
         wait.wait_recv()
     for wait in waits:
         wait.wait_send()
+
+
+def output_kernel(left_ref, right_ref, rem_ref, quot_out, rem_out):
+    half = left_ref.shape[1]
+    quot_out[:, :half] = left_ref[...].astype(jnp.float32)
+    quot_out[:, half:] = right_ref[...].astype(jnp.float32)
+    rem_out[...] = rem_ref[...]
+
+
+def write_outputs(left, right, rem):
+    rows, half = left.shape
+    tile = rows // 4
+    side = pl.BlockSpec((tile, half), lambda i: (i, 0))
+    rem_spec = pl.BlockSpec(rem.shape, lambda i: (0, 0))
+    return pl.pallas_call(
+        output_kernel,
+        grid=(rows // tile,),
+        out_shape=[
+            jax.ShapeDtypeStruct((rows, 2 * half), jnp.float32),
+            jax.ShapeDtypeStruct(rem.shape, jnp.float32),
+        ],
+        in_specs=[side, side, rem_spec],
+        out_specs=[pl.BlockSpec((tile, 2 * half), lambda i: (i, 0)), rem_spec],
+    )(left, right, rem)
 
 
 def on_device(
@@ -342,17 +397,23 @@
     wide_shape = pltpu.VMEM((wide_size, quot_slots, width), half)
     narrow_shape = pltpu.VMEM((narrow_size, rem_slots, width), half)
     block_shape = pltpu.VMEM((wide_size, block_slots, width), half)
-    part = (narrow_size, quot_rows // narrow_size, width)
+    prod_shape = pltpu.VMEM((wide_size, quot_slots, width // 2), half)
+    part = (narrow_size, quot_rows // narrow_size, width // 2)
+    anywhere = pl.BlockSpec(memory_space=pl.ANY)
     whole = pl.BlockSpec(memory_space=pltpu.VMEM)
-    copies, grad_rem = pl.pallas_call(
+    left, right, grad_rem = pl.pallas_call(
         fused_kernel,
         out_shape=[
             jax.ShapeDtypeStruct(part, half),
+            jax.ShapeDtypeStruct(part, half),
             jax.ShapeDtypeStruct((rows_each, width), jnp.float32),
         ],
-        in_specs=[whole] * 8,
-        out_specs=[pl.BlockSpec(memory_space=pl.ANY), whole],
+        in_specs=[whole] * 4 + [anywhere, anywhere, whole, anywhere],
+        out_specs=[anywhere, anywhere, whole],
         scratch_shapes=[
+            pltpu.VMEM(out_grad.shape, half),
+            pltpu.VMEM(quot_table.shape, half),
+            pltpu.VMEM(rem_table.shape, half),
             pltpu.VMEM((8, tokens), jnp.int32),
             wide_ids,
             narrow_ids,
@@ -366,8 +427,10 @@
             wide_shape,
             narrow_shape,
             narrow_shape,
-            wide_shape,
-            wide_shape,
+            prod_shape,
+            prod_shape,
+            prod_shape,
+            prod_shape,
             narrow_shape,
             narrow_shape,
             block_shape,
@@ -376,10 +439,14 @@
             pltpu.VMEM((wide_size * block_slots, tokens), half),
             pltpu.VMEM(part, half),
             pltpu.VMEM(part, half),
+            pltpu.VMEM(part, half),
+            pltpu.VMEM(part, half),
             pltpu.VMEM(part[1:], half),
-            pltpu.SemaphoreType.DMA((8 + 2 * PIECES,)),
-            pltpu.SemaphoreType.DMA((8 + 2 * PIECES,)),
-            pltpu.SemaphoreType.DMA((PIECES,)),
+            pltpu.VMEM(part[1:], half),
+            pltpu.SemaphoreType.DMA((9 + 4 * PIECES,)),
+            pltpu.SemaphoreType.DMA((9 + 4 * PIECES,)),
+            pltpu.SemaphoreType.DMA((2 * PIECES,)),
+            pltpu.SemaphoreType.DMA((3,)),
         ],
         compiler_params=pltpu.CompilerParams(collective_id=0, has_side_effects=True),
     )(
@@ -392,7 +459,10 @@
         quot_scale.reshape(-1, LANES),
         rem_table,
     )
-    return (copies.reshape(-1, width).astype(jnp.float32), grad_rem[None])
+    grad_quot, grad_rem = write_outputs(
+        left.reshape(quot_rows, -1), right.reshape(quot_rows, -1), grad_rem
+    )
+    return (grad_quot, grad_rem[None])
 
 
 def solution(mesh):

time: 84.9 us -> 78.8 us (0.928); the launches traced: 84.7 us -> 77.7 us
  Pallas kernels: 80.5 us -> 77.1 us
  other arithmetic: 2.09 us -> 0 us
  local copies, waits for them, and re-layouts: 1.47 us -> 0 us
    pallas_call x1, Pallas kernels: 80.5 us -> 73.8 us  [on_device(): pl.pallas_call(fused_kernel, out_shape=[jax.ShapeDtypeStruct(part, half),...]
    pallas_call x0 -> x1, Pallas kernels: none -> 3.28 us  [write_outputs(): pl.pallas_call(output_kernel, grid=(rows // tile,), out_shape=[jax.ShapeD...]
    convert_element_type x1 -> x0, other arithmetic: 2.09 us -> none  [on_device(): return (copies.reshape(-1, width).astype(jnp.float32), grad_rem[None])]
    unnamed x1 -> x0, local copies, waits for them, and re-layouts: 1.47 us -> none
where the time goes in v5:
time: 78.8 us; the launch traced here: 77.7 us
  Pallas kernels  77.1 us (98%)
    pallas_call x1, Pallas kernels, on_device(): pl.pallas_call(fused_kernel, out_shape=[jax.ShapeDtypeStruct(part, half),...  73.8 us
    pallas_call x1, Pallas kernels, write_outputs(): pl.pallas_call(output_kernel, grid=(rows // tile,), out_shape=[jax.ShapeD...  3.28 us

profile of v5, /device:TPU:6, one launch (start us, length us, event | category | flops | bytes accessed | tf_op | source)
XLA Modules:
  0.0 77.7 jit_solution(16753725410963299828)
XLA Ops:
  0.6 73.8 %shard_map.95 = (bf16[8,128,128]{2,1,0:T(8,128)(2,1)}, bf16[8,128,128]{2,1,0:T(8,128)(2,1)}, f32[64,256]{1,0:T(8,128)}) custom-call(s32[1,512]{1,0:T(1,128)} %bitcast.11, s32[1,512]{1,0:T(1,128)} %bitcast.12, s32[1,512]{1,0:T(1,128)} %bitcast.13, s32[1,512]{1,0:T(1,128)} %bitcast.14, bf16[512,256]{1,0:T(8,128)(2,1)} %grads_src.1, ...), custom_call_target="tpu_custom_call" | custom-call | tf_op jit(solution)/shard_map/pallas_call | solution.py:404
  74.4 3.3 %shard_map.96 = (f32[1024,256]{1,0:T(8,128)}, f32[64,256]{1,0:T(8,128)}) custom-call(bf16[1024,128]{1,0:T(8,128)(2,1)} %bitcast.8, bf16[1024,128]{1,0:T(8,128)(2,1)} %bitcast.9, f32[64,256]{1,0:T(8,128)} %get-tuple-element.9.rem_ref), custom_call_target="tpu_custom_call" | custom-call | tf_op jit(solution)/shard_map/pallas_call | solution.py:371

commit v6 on v5

--- a/solution.py
+++ b/solution.py
@@ -12,6 +12,7 @@
 AXES = ("wide", "narrow")
 LANES = 128
 PIECES = 2
+STRIDES = {"wide": 27, "narrow": 3}
 
 
 def greet_peers():
@@ -34,7 +35,7 @@
     size, me = lax.axis_size(axis), lax.axis_index(axis)
 
     def send(step, carry):
-        peer = lax.rem(me + step, size)
+        peer = lax.rem(me + step * STRIDES[axis], size)
         pltpu.make_async_remote_copy(
             src_ref=pick(peer),
             dst_ref=land(dst, me),
@@ -365,7 +366,7 @@
 
 def write_outputs(left, right, rem):
     rows, half = left.shape
-    tile = rows // 4
+    tile = rows // 2
     side = pl.BlockSpec((tile, half), lambda i: (i, 0))
     rem_spec = pl.BlockSpec(rem.shape, lambda i: (0, 0))
     return pl.pallas_call(

time: 78.8 us -> 77.5 us (0.984)
  Pallas kernels: 77.1 us -> 75.7 us
    pallas_call x1, Pallas kernels: 3.28 us -> 2.02 us  [write_outputs(): pl.pallas_call(output_kernel, grid=(rows // tile,), out_shape=[jax.ShapeD...]
where the time goes in v6:
time: 77.5 us; the launch traced here: 76.4 us
  Pallas kernels  75.7 us (98%)
    pallas_call x1, Pallas kernels, on_device(): pl.pallas_call(fused_kernel, out_shape=[jax.ShapeDtypeStruct(part, half),...  73.7 us
    pallas_call x1, Pallas kernels, write_outputs(): pl.pallas_call(output_kernel, grid=(rows // tile,), out_shape=[jax.ShapeD...  2.02 us

profile of v6, /device:TPU:6, one launch (start us, length us, event | category | flops | bytes accessed | tf_op | source)
XLA Modules:
  0.0 76.4 jit_solution(4671338823078421645)
XLA Ops:
  0.6 73.7 %shard_map.95 = (bf16[8,128,128]{2,1,0:T(8,128)(2,1)}, bf16[8,128,128]{2,1,0:T(8,128)(2,1)}, f32[64,256]{1,0:T(8,128)}) custom-call(s32[1,512]{1,0:T(1,128)} %bitcast.11, s32[1,512]{1,0:T(1,128)} %bitcast.12, s32[1,512]{1,0:T(1,128)} %bitcast.13, s32[1,512]{1,0:T(1,128)} %bitcast.14, bf16[512,256]{1,0:T(8,128)(2,1)} %grads_src.1, ...), custom_call_target="tpu_custom_call" | custom-call | tf_op jit(solution)/shard_map/pallas_call | solution.py:405
  74.3 2.0 %shard_map.96 = (f32[1024,256]{1,0:T(8,128)}, f32[64,256]{1,0:T(8,128)}) custom-call(bf16[1024,128]{1,0:T(8,128)(2,1)} %bitcast.8, bf16[1024,128]{1,0:T(8,128)(2,1)} %bitcast.9, f32[64,256]{1,0:T(8,128)} %get-tuple-element.9.rem_ref), custom_call_target="tpu_custom_call" | custom-call | tf_op jit(solution)/shard_map/pallas_call | solution.py:372
